TPU v7x, 256 devices: a whole 4x4x8 slice. The times are simulated.
256 devices in a mesh: leaf: 128 (over x, y, z), col: 2 (over core).
Axes of the slice: x: 4, y: 4, z: 8, core: 2. Of those that a mesh axis runs over, the one named last changes fastest.
Arguments:
- coords: float32 [3, 262144], P(None, 'leaf'), may hold values from -6 to 6
- values: float32 [32, 262144], P('col', 'leaf'), may hold values from -6 to 6
- leaf_basis: float32 [1024, 256, 128], P('leaf'), may hold values from -0.375 to 0.375
- leaf_transfer: float32 [1024, 128, 128], P('leaf'), may hold values from -0.1875 to 0.1875
- node_transfer: float32 [128, 128, 128], P('leaf'), may hold values from -0.1875 to 0.1875
- leaf_coupling: float32 [1024, 8, 128, 128], P('leaf', None, 'col'), may hold values from -0.1875 to 0.1875
- node_coupling: float32 [128, 2, 128, 128], P('leaf', None, 'col'), may hold values from -0.375 to 0.375
- top_coupling: float32 [16, 4, 128, 128], P(None, None, 'col'), may hold values from -0.25 to 0.25
- near_list: int32 [1024, 8], P('leaf'), may hold values from -1 to 1023, as said below
- leaf_list: int32 [1024, 8], P('leaf'), may hold values from -1 to 1023, as said below
- node_list: int32 [128, 2], P('leaf'), may hold values from -1 to 127, as said below
- top_list: int32 [16, 4], replicated, may hold values from -1 to 15, as said below
Outputs:
- adjoint_product: float32 [32, 262144], P('col', 'leaf')
Inputs may be any that keep to these rules, and one draw needn't show every extreme that they name: `leaf_list`: leaf l names only leaves other than itself on devices l // 8 - 1 to l // 8 + 1 of a Morton order of 8 leaves a device; slot 0 is live, live slots come first, and some leaf fills all 8 slots. `near_list`: leaf l names only leaves (itself allowed) on devices l // 8 - 1 to l // 8 + 1; slot 0 is live, live slots come first, and some leaf fills all 8 slots. `node_list`: node p names only nodes p - 1 and p + 1; slot 0 is live, live slots come first, and some node fills all 2 slots. `top_list`: top node g may name any top node, itself allowed; slot 0 is live, live slots come first, and some top node fills all 4 slots.
All inputs are finite; a program needn't handle non-finite values.
Results may differ from a plain program's by a relative error of at most 0.0003.
Values sent between devices are 32-bit elements; how exact they have to be, the bound alone decides.
A program may use at most 64 MiB of HBM per device.

v0:
```python
import math

import jax
import jax.numpy as jnp
from jax import lax
from jax.sharding import PartitionSpec as P

SOFTENING = 0.01


def extended_2(x, sides, width):
    for axis, dim in sides:
        devices, length = (lax.axis_size(axis), x.shape[dim])
        up = [(i, (i + 1) % devices) for i in range(devices - 1)]
        down = [(j, i) for i, j in up]
        last = lax.slice_in_dim(x, length - width, length, axis=dim)
        leading = lax.slice_in_dim(x, 0, width, axis=dim)
        before = lax.ppermute(last, axis, up)
        after = lax.ppermute(leading, axis, down)
        x = jnp.concatenate([before, x, after], axis=dim)
    return x


def couple(blocks, local_index, sources):
    high = lax.Precision.HIGHEST
    live_mask = (local_index >= 0).astype(jnp.float32)
    safe_index = jnp.maximum(local_index, 0)
    wide_moments = lax.all_gather(sources, "col", axis=1, tiled=True)
    half_rank = blocks.shape[2]
    rank_start = lax.axis_index("col") * half_rank
    rank_part = lax.dynamic_slice_in_dim(wide_moments, rank_start, half_rank, 2)
    picked = jnp.take(rank_part, safe_index, axis=0) * live_mask[:, :, None, None]
    partial_value = jnp.einsum("nsca,nsab->ncb", picked, blocks, precision=high)
    return lax.psum_scatter(partial_value, "col", scatter_dimension=1, tiled=True)


def body(
    coords,
    values,
    leaf_basis,
    leaf_transfer,
    node_transfer,
    leaf_coupling,
    node_coupling,
    top_coupling,
    near_list,
    leaf_list,
    node_list,
    top_list,
):
    high = lax.Precision.HIGHEST
    device = lax.axis_index("leaf")
    per_device = leaf_basis.shape[0]
    points = leaf_basis.shape[1]
    core_cols = values.shape[0]
    rank_width = leaf_basis.shape[2]
    leaf_values = values.reshape(core_cols, per_device, points)
    leaf_moments = jnp.einsum("lpr,clp->lcr", leaf_basis, leaf_values, precision=high)
    node_moments = jnp.einsum("lab,lca->cb", leaf_transfer, leaf_moments, precision=high)[None]
    contrib = jnp.einsum("nab,nca->ncb", node_transfer, node_moments, precision=high)
    top_count = lax.axis_size("leaf") // 8
    everything = lax.all_gather(contrib, "leaf", axis=0, tiled=True)
    top_moments = everything.reshape(top_count, 8, core_cols, rank_width).sum(axis=1)
    top_node = device // 8
    top_rows = lax.dynamic_slice_in_dim(top_coupling, top_node, 1, 0)
    top_index = lax.dynamic_slice_in_dim(top_list, top_node, 1, 0)
    top_local = couple(top_rows, top_index, top_moments)
    node_ext = extended_2(node_moments, (("leaf", 0),), 1)
    node_index = jnp.where(node_list >= 0, node_list - (device - 1), -1)
    node_local = couple(node_coupling, node_index, node_ext) + jnp.einsum(
        "nab,ncb->nca", node_transfer, top_local, precision=high
    )
    leaf_ext = extended_2(leaf_moments, (("leaf", 0),), per_device)
    leaf_index = jnp.where(leaf_list >= 0, leaf_list - (device - 1) * per_device, -1)
    leaf_local = couple(leaf_coupling, leaf_index, leaf_ext) + jnp.einsum(
        "lab,cb->lca", leaf_transfer, node_local[0], precision=high
    )
    far_field = jnp.einsum("lpr,lcr->clp", leaf_basis, leaf_local, precision=high)
    leaf_rows = jnp.concatenate((coords, values), axis=0)
    extended = extended_2(leaf_rows, (("leaf", 1),), per_device * points)
    extended = extended.reshape(3 + core_cols, 3 * per_device, points)
    near_index = jnp.where(near_list >= 0, near_list - (device - 1) * per_device, -1)
    target = coords.reshape(3, per_device, points)
    scale = 1.0 / math.sqrt(points)
    near_field = jnp.zeros((per_device, core_cols, points), jnp.float32)
    for slot_index in range(near_list.shape[1]):
        column = near_index[:, slot_index]
        live_mask = (column >= 0).astype(jnp.float32)
        source_rows = jnp.take(extended, jnp.maximum(column, 0), axis=1)
        offset_sq = jnp.sum((target[:, :, :, None] - source_rows[:3, :, None, :]) ** 2, axis=0)
        kernel = scale / jnp.sqrt(offset_sq + SOFTENING)
        term = jnp.einsum("lab,clb->lca", kernel, source_rows[3:], precision=high)
        near_field = near_field + live_mask[:, None, None] * term
    total = jnp.transpose(near_field, (1, 0, 2)) + far_field
    return total.reshape(core_cols, per_device * points)


def solution(mesh):
    in_specs = (
        P(None, "leaf"),
        P("col", "leaf"),
        P("leaf", None, None),
        P("leaf", None, None),
        P("leaf", None, None),
        P("leaf", None, "col", None),
        P("leaf", None, "col", None),
        P(None, None, "col", None),
        P("leaf", None),
        P("leaf", None),
        P("leaf", None),
        P(),
    )
    out_specs = P("col", "leaf")
    return jax.shard_map(body, mesh=mesh, in_specs=in_specs, out_specs=out_specs, check_vma=False)
```

profile of v0, /device:TPU:1, one launch (start us, length us, event | category | flops | bytes accessed | tf_op | source)
XLA Modules:
  0.0 207.8 jit_solution(12631651173582469412)
XLA Ops:
  7.5 1.8 pad_maximum_fusion.1
  9.2 5.0 %collective-permute-start = (f32[19,2048]{1,0:T(8,128)}, f32[19,2048]{1,0:T(8,128)}, u32[]{:S(2)}, u32[]{:S(2)}) collective-permute-start(f32[19,2048]{1,0:T(8,128)} %pad_maximum_fusion.1), channel_id=1, source_target_pairs={{0,2},{2,4},{4,6},{6,8},{8,10},{10,12},{12,14},{14,16},{16,18},{18... | collective-permute-start | bytes 466952 | tf_op jit(solution)/shard_map/ppermute | solution.py:18
  15.5 1.9 fusion.107
  17.5 1.4 fusion.159
  18.9 4.0 %collective-permute-start.4 = (f32[1,16,128]{2,1,0:T(8,128)S(1)}, f32[1,16,128]{2,1,0:T(8,128)S(1)}, u32[]{:S(2)}, u32[]{:S(2)}) collective-permute-start(f32[1,16,128]{2,1,0:T(8,128)S(1)} %bitcast.94), channel_id=1, source_target_pairs={{0,2},{2,4},{4,6},{6,8},{8,10},{10,12},{12,14},{14,16},{16,18},{18... | collective-permute-start | bytes 24584 | tf_op jit(solution)/shard_map/ppermute | solution.py:18
  24.2 4.0 %collective-permute-start.2 = (f32[8,16,128]{2,1,0:T(8,128)S(1)}, f32[8,16,128]{2,1,0:T(8,128)S(1)}, u32[]{:S(2)}, u32[]{:S(2)}) collective-permute-start(f32[8,16,128]{2,1,0:T(8,128)S(1)} %fusion.107), channel_id=1, source_target_pairs={{0,2},{2,4},{4,6},{6,8},{8,10},{10,12},{12,14},{14,16},{16,18},{18... | collective-permute-start | bytes 196616 | tf_op jit(solution)/shard_map/ppermute | solution.py:18
  41.6 3.6 %all_gather.13 = f32[3,32,128]{2,1,0:T(8,128)S(1)} all-gather(f32[3,16,128]{2,1,0:T(8,128)S(1)} %pad_maximum_fusion.3), channel_id=1, replica_groups=mesh['leaf'=128,'col'=2] {'col'}, dimensions={1}, use_global_device_ids=true | all-gather | bytes 73728 | tf_op jit(solution)/shard_map/all_gather | solution.py:28
  46.8 3.7 %all_gather.12 = f32[24,32,128]{2,1,0:T(8,128)S(1)} all-gather(f32[24,16,128]{2,1,0:T(8,128)S(1)} %pad_maximum_fusion.2), channel_id=1, replica_groups=mesh['leaf'=128,'col'=2] {'col'}, dimensions={1}, use_global_device_ids=true | all-gather | bytes 589824 | tf_op jit(solution)/shard_map/all_gather | solution.py:28
  51.3 84.4 %all-gather.3.cloned.1.call-done = f32[2048,128]{1,0:T(8,128)} async-done(((f32[16,128]{1,0:T(8,128)}), f32[2048,128]{1,0:T(8,128)}) %all-gather.3.cloned.1.call-update) | async-done | bytes 1048592 | tf_op jit(solution)/shard_map/all_gather | solution.py:62
  135.7 1.3 reduce_sum.89
  137.0 7.1 %all_gather.15 = f32[16,32,128]{2,1,0:T(8,128)S(1)} all-gather(f32[16,16,128]{2,1,0:T(8,128)S(1)} %reduce_sum.89), channel_id=1, replica_groups=mesh['leaf'=128,'col'=2] {'col'}, dimensions={1}, use_global_device_ids=true | all-gather | bytes 393216 | tf_op jit(solution)/shard_map/all_gather | solution.py:28
  144.3 1.3 gather_fusion.2
  145.6 1.9 convolution_bitcast_fusion.2
  147.5 2.1 %convolution_bitcast_fusion = f32[8,32,128]{2,1,0:T(8,128)} fusion(f32[8,8,64,128]{3,2,1,0:T(8,128)S(1)} %copy-done, f32[8,8,32,64]{3,2,1,0:T(8,128)S(1)} %bitcast.87, f32[8,8]{1,0:T(8,128)S(1)} %get-tuple-element.34, pred[8,8]{1,0:T(8,128)(4,1)S(1)} %copy-done.17), kind=kOutput, calls=%fused_computation.68 | convolution fusion | flops 201588736 | bytes 2752832 | tf_op jit(solution)/shard_map/nsca,nsab->ncb/dot_general | solution.py:33
  167.2 11.0 %multiply_reduce_fusion = (f32[8,256,256]{2,1,0:T(8,128)}, f32[8,256,256]{2,1,0:T(8,128)S(1)}, f32[8,256,256]{2,1,0:T(8,128)S(1)}, f32[8,256,256]{2,1,0:T(8,128)...) fusion(f32[3,8,256]{2,1,0:T(8,128)S(1)} %copy.65, ...), kind=kLoop, calls=%fused_computation.11 | loop fusion | flops 33554432 | bytes 16998400 | tf_op jit(solution)/shard_map/reduce_sum | solution.py:90
  178.3 1.9 fusion.44
  180.2 1.9 fusion.47
  182.1 1.9 fusion.50
  184.1 1.9 fusion.65
  186.0 1.9 fusion.68
  187.9 1.9 fusion.41
  189.9 2.6 %fusion.62 = f32[8,16,256]{2,1,0:T(8,128)} fusion(f32[8,16,256]{2,1,0:T(8,128)S(1)} %fusion.68, f32[8,16,256]{2,1,0:T(8,128)S(1)} %fusion.65, f32[8,16,256]{2,1,0:T(8,128)S(1)} %fusion.41, f32[8,256,256]{2,1,0:T(8,128)S(1)} %get-tuple-element.10, f32[19,8,256]{2,0,1:T(8,128)S(1)} %select_bitcast_fusion.3, f32[8]{0:T(128)S(1)} %copy-done.20), kind=kOutput, calls=%fused_computation.61 | convolution fusion | flops 101842944 | bytes 2753024 | tf_op jit(solution)/shard_map/lab,clb->lca/dot_general | solution.py:92
  193.5 1.6 fusion.83
  196.1 3.5 %fusion.80 = f32[8,2,8,256]{3,2,1,0:T(8,128)S(1)} fusion(f32[8,16,256]{2,1,0:T(8,128)S(1)} %fusion.160, f32[8,16,256]{2,1,0:T(8,128)} %fusion.62, f32[8,256,256]{2,1,0:T(8,128)} %get-tuple-element.6, f32[19,8,256]{2,0,1:T(8,128)S(1)} %select_bitcast_fusion, f32[8]{0:T(128)S(1)} %copy-done.32), kind=kOutput, calls=%fused_computation.67 | convolution fusion | flops 101810176 | bytes 2621952 | tf_op jit(solution)/shard_map/lab,clb->lca/dot_general | solution.py:92
  (168 shorter events, 38.5 us)
Async XLA Ops:
  7.4 140.1 %copy-start = (f32[8,8,64,128]{3,2,1,0:T(8,128)S(1)}, f32[8,8,64,128]{3,2,1,0:T(8,128)}, u32[]{:S(2)}) copy-start(f32[8,8,64,128]{3,2,1,0:T(8,128)} %param.19) | copy-start | bytes 6291460
  7.4 30.8 %copy-start.11 = (f32[3,2048]{1,0:T(4,128)S(1)}, f32[3,2048]{1,0:T(4,128)}, u32[]{:S(2)}) copy-start(f32[3,2048]{1,0:T(4,128)} %param.14) | copy-start | bytes 73732
  7.4 20.8 %copy-start.13 = (f32[1,128,128]{2,1,0:T(8,128)S(1)}, f32[1,128,128]{2,1,0:T(8,128)}, u32[]{:S(2)}) copy-start(f32[1,128,128]{2,1,0:T(8,128)} %param.18) | copy-start | bytes 196612
  7.4 21.7 %copy-start.19 = (s32[8,8]{1,0:T(8,128)S(1)}, s32[8,8]{1,0:T(8,128)}, u32[]{:S(2)}) copy-start(s32[8,8]{1,0:T(8,128)} %param.22) | copy-start | bytes 772
  7.4 25.6 %copy-start.16 = (s32[16,4]{0,1:T(4,128)S(1)}, s32[16,4]{0,1:T(4,128)}, u32[]{:S(2)}) copy-start(s32[16,4]{0,1:T(4,128)} %param.25) | copy-start | bytes 772
  7.4 26.4 %copy-start.33 = (s32[1,2]{1,0:T(1,128)S(1)}, s32[1,2]{1,0:T(1,128)}, u32[]{:S(2)}) copy-start(s32[1,2]{1,0:T(1,128)} %param.24) | copy-start | bytes 28
  7.4 26.4 %copy-start.18 = (s32[8,8]{1,0:T(8,128)S(1)}, s32[8,8]{1,0:T(8,128)}, u32[]{:S(2)}) copy-start(s32[8,8]{1,0:T(8,128)} %param.23) | copy-start | bytes 772
  7.4 38.4 %copy-start.15 = (f32[1,2,64,128]{3,2,1,0:T(8,128)S(1)}, f32[1,2,64,128]{3,2,1,0:T(8,128)}, u32[]{:S(2)}) copy-start(f32[1,2,64,128]{3,2,1,0:T(8,128)} %param.20) | copy-start | bytes 196612
  7.4 128.3 %all-gather.3.cloned.1.call-start = ((), (), s32[]{:S(2)}) async-start(), calls=%async_computation.6 | async-start | bytes 1056768 | tf_op jit(solution)/shard_map/all_gather | solution.py:62
  9.2 140.5 %collective-permute-start = (f32[19,2048]{1,0:T(8,128)}, f32[19,2048]{1,0:T(8,128)}, u32[]{:S(2)}, u32[]{:S(2)}) collective-permute-start(f32[19,2048]{1,0:T(8,128)} %pad_maximum_fusion.1), channel_id=1, source_target_pairs={{0,2},{2,4},{4,6},{6,8},{8,10},{10,12},{12,14},{14,16},{16,18},{18... | collective-permute-start | bytes 466952 | tf_op jit(solution)/shard_map/ppermute | solution.py:18
  14.3 135.5 %collective-permute-start.1 = (f32[19,2048]{1,0:T(8,128)}, f32[19,2048]{1,0:T(8,128)}, u32[]{:S(2)}, u32[]{:S(2)}) collective-permute-start(f32[19,2048]{1,0:T(8,128)} %pad_maximum_fusion.1), channel_id=1, source_target_pairs={{2,0},{4,2},{6,4},{8,6},{10,8},{12,10},{14,12},{16,14},{18,16},{20... | collective-permute-start | bytes 466952 | tf_op jit(solution)/shard_map/ppermute | solution.py:19
  18.9 21.4 %collective-permute-start.4 = (f32[1,16,128]{2,1,0:T(8,128)S(1)}, f32[1,16,128]{2,1,0:T(8,128)S(1)}, u32[]{:S(2)}, u32[]{:S(2)}) collective-permute-start(f32[1,16,128]{2,1,0:T(8,128)S(1)} %bitcast.94), channel_id=1, source_target_pairs={{0,2},{2,4},{4,6},{6,8},{8,10},{10,12},{12,14},{14,16},{16,18},{18... | collective-permute-start | bytes 24584 | tf_op jit(solution)/shard_map/ppermute | solution.py:18
  22.9 18.7 %collective-permute-start.5 = (f32[1,16,128]{2,1,0:T(8,128)S(1)}, f32[1,16,128]{2,1,0:T(8,128)S(1)}, u32[]{:S(2)}, u32[]{:S(2)}) collective-permute-start(f32[1,16,128]{2,1,0:T(8,128)S(1)} %bitcast.95), channel_id=1, source_target_pairs={{2,0},{4,2},{6,4},{8,6},{10,8},{12,10},{14,12},{16,14},{18,16},{20... | collective-permute-start | bytes 24584 | tf_op jit(solution)/shard_map/ppermute | solution.py:19
  24.2 22.6 %collective-permute-start.2 = (f32[8,16,128]{2,1,0:T(8,128)S(1)}, f32[8,16,128]{2,1,0:T(8,128)S(1)}, u32[]{:S(2)}, u32[]{:S(2)}) collective-permute-start(f32[8,16,128]{2,1,0:T(8,128)S(1)} %fusion.107), channel_id=1, source_target_pairs={{0,2},{2,4},{4,6},{6,8},{8,10},{10,12},{12,14},{14,16},{16,18},{18... | collective-permute-start | bytes 196616 | tf_op jit(solution)/shard_map/ppermute | solution.py:18
  29.0 163.4 %reduce-scatter.6.cloned.1.call-start = ((), (), s32[]{:S(2)}) async-start(), calls=%async_computation.4 | async-start | bytes 24576 | tf_op jit(solution)/shard_map/reduce_scatter | solution.py:34
  40.3 6.5 %collective-permute-start.3 = (f32[8,16,128]{2,1,0:T(8,128)S(1)}, f32[8,16,128]{2,1,0:T(8,128)S(1)}, u32[]{:S(2)}, u32[]{:S(2)}) collective-permute-start(f32[8,16,128]{2,1,0:T(8,128)S(1)} %fusion.107), channel_id=1, source_target_pairs={{2,0},{4,2},{6,4},{8,6},{10,8},{12,10},{14,12},{16,14},{18,16},{20... | collective-permute-start | bytes 196616 | tf_op jit(solution)/shard_map/ppermute | solution.py:19
  46.7 145.7 %reduce-scatter.8.cloned.1.call-start = ((), (), s32[]{:S(2)}) async-start(), calls=%async_computation.5 | async-start | bytes 24576 | tf_op jit(solution)/shard_map/reduce_scatter | solution.py:34
  51.3 96.2 %copy-start.17 = (pred[8,8]{1,0:T(8,128)(4,1)S(1)}, pred[8,8]{1,0:T(8,128)(4,1)}, u32[]{:S(2)}) copy-start(pred[8,8]{1,0:T(8,128)(4,1)} %get-tuple-element.32) | copy-start | bytes 196
  147.5 46.0 %reduce-scatter.4.cloned.1.call-start = ((), (), s32[]{:S(2)}) async-start(), calls=%async_computation.3 | async-start | bytes 196608 | tf_op jit(solution)/shard_map/reduce_scatter | solution.py:34
  151.1 7.8 %copy-start.28 = (pred[8]{0:T(512)(128)(4,1)S(1)}, pred[8]{0:T(512)(128)(4,1)}, u32[]{:S(2)}) copy-start(pred[8]{0:T(512)(128)(4,1)} %get-tuple-element.44) | copy-start | bytes 28
  152.0 9.0 %copy-start.27 = (pred[8]{0:T(512)(128)(4,1)S(1)}, pred[8]{0:T(512)(128)(4,1)}, u32[]{:S(2)}) copy-start(pred[8]{0:T(512)(128)(4,1)} %get-tuple-element.43) | copy-start | bytes 28
  155.6 11.6 %copy-start.14 = (f32[1,3,8,256]{3,2,1,0:T(8,128)S(1)}, f32[1,3,8,256]{3,2,1,0:T(8,128)}, u32[]{:S(2)}) copy-start(f32[1,3,8,256]{3,2,1,0:T(8,128)} %copy.78) | copy-start | bytes 73732
  167.2 11.0 %copy-start.26 = (f32[8]{0:T(128)S(1)}, f32[8]{0:T(128)}, u32[]{:S(2)}) copy-start(f32[8]{0:T(128)} %get-tuple-element.20) | copy-start | bytes 100
  189.8 6.2 %copy-start.32 = (f32[8]{0:T(128)S(1)}, f32[8]{0:T(128)}, u32[]{:S(2)}) copy-start(f32[8]{0:T(128)} %get-tuple-element.14) | copy-start | bytes 100
  (20 other events, 62.9 us)
Sparse Core Ops, SparseCore 0:
  29.1 106.5 all-gather.2
Sparse Core Ops, SparseCore 1:
  46.8 21.7 reduce-scatter.5
  147.5 12.2 reduce-scatter.7
  162.2 14.1 reduce-scatter.3
where the time goes:
time: 209 us; the launch traced here: 208 us
  waiting for transfers between devices  84.5 us (40%)
  matrix products  30 us (14%)
  other arithmetic  28.5 us (14%)
  local copies, waits for them, and re-layouts  17.6 us (8%)
  starting transfers between devices  17 us (8%)
  between operations  15.8 us (8%)
  blocking collectives  14.3 us (7%)
    all_gather x1, waiting for transfers between devices, body(): everything = lax.all_gather(contrib, 'leaf', axis=0, tiled=True)  84.4 us
    dot_general x8, matrix products, body(): term = jnp.einsum('lab,clb->lca', kernel, source_rows[3:], precision=high)  17.4 us
    all_gather x3, blocking collectives, couple(): wide_moments = lax.all_gather(sources, 'col', axis=1, tiled=True)  14.3 us
    ppermute x3, starting transfers between devices, extended_2(): before = lax.ppermute(last, axis, up)  13 us
    reduce_sum x1, other arithmetic, body(): jnp.sum((target[:, :, :, None] - source_rows[:3, :, None, :]) ** 2, axis=0)  11 us
    gather x8, local copies, waits for them, and re-layouts, body(): source_rows = jnp.take(extended, jnp.maximum(column, 0), axis=1)  5.88 us
    dot_general x3, matrix products, couple(): partial_value = jnp.einsum('nsca,nsab->ncb', picked, blocks, precision=high)  4.92 us
    slice x16, local copies, waits for them, and re-layouts, body(): source_rows[:3, :, None, :]  4.28 us
  transfers between devices with their start and end apart: 10, of which 2 were waited for; matrix products, arithmetic and copies ran while one was open for 31% of the time, Pallas kernels for 0%

commit v1 on v0

v1 whole, which is shorter than its diff:
```python
import functools

import jax
import jax.numpy as jnp
from jax import lax
from jax.experimental import pallas as pl
from jax.experimental.pallas import tpu as pltpu
from jax.sharding import PartitionSpec as P

SOFTENING = 0.01
F32, BF16 = jnp.float32, jnp.bfloat16
MESH = pl.DeviceIdType.MESH
NN = (((1,), (0,)), ((), ()))
NT = (((1,), (1,)), ((), ()))


def mm(a, b, dims):
    return lax.dot_general(a, b, dims, preferred_element_type=F32)


def split(x):
    hi = x.astype(BF16)
    return hi, (x - hi.astype(F32)).astype(BF16)


def stacked(x):
    return jnp.concatenate(split(x), axis=0)


def dot3(x2, yh, yl, dims):
    m = x2.shape[0] // 2
    both = mm(x2, yh, dims)
    return both[:m] + both[m:] + mm(x2[:m], yl, dims)


def kernel(
    near_ref, leaf_ref, node_ref, top_ref, coords,
    values_hbm, basis_hbm, ltr_hbm, ntr_hbm, lcp_hbm, ncp_hbm, tcp_hbm,
    out,
    vals, ev, cs, vs, bx, em, en, zb, tb, sm, sn, sc, st,
    basis, ltr, ntr, lcp, ncp, tcp, bh, bl, lth, ltl, nth, ntl,
    ox, sx, rx, sp, rp,
    local_sem, v_send, v_recv, c_send, c_recv, m_send, m_recv, n_send, n_recv,
    z_send, z_recv, t_send, t_recv, x_send, x_recv,
):
    leaves, chips = 8, 128
    cols = vals.shape[0]
    d, c = lax.axis_index("leaf"), lax.axis_index("col")
    o = 1 - c
    z, g = lax.rem(d, 8), lax.div(d, 8)
    after, before = lax.rem(d + 1, chips), lax.rem(d + chips - 1, chips)

    def fetch(i, src, dst):
        copy = pltpu.make_async_copy(src, dst, local_sem.at[i])
        copy.start()
        return copy

    get_values = fetch(0, values_hbm, vals)
    get_basis = fetch(1, basis_hbm, basis)
    get_ltr = fetch(2, ltr_hbm, ltr)
    get_ntr = fetch(3, ntr_hbm, ntr)
    get_lcp = fetch(4, lcp_hbm, lcp)
    get_ncp = fetch(5, ncp_hbm, ncp)
    get_tcp = fetch(6, tcp_hbm.at[g], tcp)

    barrier = pltpu.get_barrier_semaphore()

    def greet(leaf, col):
        pl.semaphore_signal(barrier, inc=1, device_id=(leaf, col), device_id_type=MESH)

    greet(d, o)
    for h in range(2):
        greet(after, h)
        greet(before, h)
        for k in range(1, 8):
            greet(g * 8 + lax.rem(z + k, 8), h)
    for k in range(1, 16):
        greet(lax.rem(g + k, 16) * 8 + z, c)

    def remote(src, dst, ssem, rsem, leaf, col):
        return pltpu.make_async_remote_copy(
            src_ref=src, dst_ref=dst, send_sem=ssem, recv_sem=rsem,
            device_id=(leaf, col), device_id_type=MESH,
        )

    zero8 = jnp.zeros((8, 128), F32)
    for l in range(leaves):
        for h in range(2):
            start = l * 256 + h * 128
            cs[leaves + l, 3 * h : 3 * h + 3, :] = coords[:, start : start + 128]
        cs[leaves + l, 6:8, :] = zero8[:2]
    cs[24] = zero8
    vs[24] = jnp.zeros((2 * cols, 256), BF16)
    for s in range(2):
        em[s, 24] = zero8
        en[s, 3] = zero8
        tb[16, s] = zero8
    get_values.wait()
    for l in range(leaves):
        vs[leaves + l] = stacked(vals[:, l * 256 : (l + 1) * 256])

    pl.semaphore_wait(barrier, 34)
    sends = []

    def send(*args):
        copy = remote(*args)
        copy.start()
        sends.append(copy)

    for q, leaf in ((0, after), (1, before)):
        send(vals, ev.at[q], v_send.at[q], v_recv.at[q], leaf, c)
        send(cs.at[pl.ds(leaves, leaves)], cs.at[pl.ds(16 * q, leaves)], c_send.at[q], c_recv.at[q], leaf, c)

    low = lax.broadcasted_iota(jnp.int32, (8, 128), 1) < 64

    def half(x, h):
        a, b = x[:8], x[8:]
        return jnp.where(low, a, pltpu.roll(b, 64, 1)) if h == 0 else jnp.where(low, pltpu.roll(a, 64, 1), b)

    get_basis.wait()
    get_ltr.wait()
    get_ntr.wait()
    nth[...], ntl[...] = split(ntr[0])
    node = None
    for l in range(leaves):
        hi, lo = split(basis[l])
        bh[l], bl[l] = hi, lo
        moments = dot3(vs[leaves + l], hi, lo, NN)
        for h in range(2):
            sm[h, l] = half(moments, h)
        thi, tlo = split(ltr[l])
        lth[l], ltl[l] = thi, tlo
        term = dot3(stacked(moments), thi, tlo, NN)
        node = term if node is None else node + term
    contrib = dot3(stacked(node), nth[...], ntl[...], NN)
    for h in range(2):
        sn[h] = half(node, h)
        sc[h] = half(contrib, h)

    send(sc.at[o], zb.at[0, c], z_send.at[0, o], z_recv.at[0, c], d, o)
    for k in range(1, 8):
        for h in range(2):
            send(sc.at[h], zb.at[k, c], z_send.at[k, h], z_recv.at[k, c], g * 8 + lax.rem(z + k, 8), h)
    zb[0, c] = sc[c]
    send(sm.at[o], em.at[c, pl.ds(leaves, leaves)], m_send.at[2, o], m_recv.at[1, c], d, o)
    send(sn.at[o], en.at[c, 1], n_send.at[2, o], n_recv.at[1, c], d, o)
    for q, leaf in ((0, after), (1, before)):
        for h in range(2):
            send(sn.at[h], en.at[c, 2 * q], n_send.at[q, h], n_recv.at[2 * q, c], leaf, h)
            send(sm.at[h], em.at[c, pl.ds(16 * q, leaves)], m_send.at[q, h], m_recv.at[2 * q, c], leaf, h)
    em[c, pl.ds(leaves, leaves)] = sm[c]
    en[c, 1] = sn[c]

    for q in range(2):
        remote(vals, ev.at[q], v_send.at[q], v_recv.at[q], after, c).wait_recv()
        mine = cs.at[pl.ds(16 * q, leaves)]
        remote(mine, mine, c_send.at[q], c_recv.at[q], after, c).wait_recv()
        for l in range(leaves):
            vs[16 * q + l] = stacked(ev[q, :, l * 256 : (l + 1) * 256])

    def source(v, per, none):
        return jnp.where(v >= 0, jnp.clip(v - (d - 1) * per, 0, none - 1), none)

    def near(l, carry):
        points = cs[leaves + l].T
        for k in range(3):
            bx[k, 0:128, :] = jnp.broadcast_to(points[:, k : k + 1], (128, 128))
            bx[k, 128:256, :] = jnp.broadcast_to(points[:, 3 + k : 4 + k], (128, 128))
        total = None
        for j in range(8):
            i = source(near_ref[l, j], leaves, 24)
            rows = cs[i]
            his, los = [], []
            for h in range(2):
                r2 = None
                for k in range(3):
                    e = bx[k] - rows[3 * h + k : 3 * h + k + 1, :]
                    r2 = e * e if r2 is None else r2 + e * e
                hi, lo = split(lax.rsqrt(r2 + SOFTENING))
                his.append(hi)
                los.append(lo)
            term = dot3(vs[i], jnp.concatenate(his, 1), jnp.concatenate(los, 1), NT)
            total = term if total is None else total + term
        out[:, pl.ds(pl.multiple_of(l * 256, 256), 256)] = total * (1.0 / 16.0)
        return carry

    lax.fori_loop(0, 3, near, 0)

    for k in range(8):
        for s in range(2):
            if k == 0:
                continue
            remote(sc.at[0], zb.at[k, s], z_send.at[k, s], z_recv.at[k, s], d, o).wait_recv()
    remote(sc.at[0], zb.at[0, o], z_send.at[0, o], z_recv.at[0, o], d, o).wait_recv()
    total = zb[0]
    for k in range(1, 8):
        total = total + zb[k]
    st[...] = total
    for k in range(1, 16):
        send(st, tb.at[g], t_send.at[k], t_recv.at[k], lax.rem(g + k, 16) * 8 + z, c)
    tb[g] = total

    def paired(load, i, j):
        rows = []
        for s in range(2):
            a, b = load(s, i), load(s, j)
            rows += [jnp.where(low, a, pltpu.roll(b, 64, 1)), jnp.where(low, pltpu.roll(a, 64, 1), b)]
        return jnp.concatenate(rows, 0)

    def coupled(load, index, blocks):
        slots = blocks.shape[0]
        picked = jnp.concatenate([paired(load, index(j), index(j + 1)) for j in range(0, slots, 2)], 1)
        return dot3(stacked(picked), *split(blocks.reshape(slots * 64, 128)), NN)

    for h in range(2):
        for q in (0, 2):
            remote(sm.at[h], em.at[h, pl.ds(8 * q, leaves)], m_send.at[0, h], m_recv.at[q, h], d, o).wait_recv()
            remote(sn.at[h], en.at[h, q], n_send.at[0, h], n_recv.at[q, h], d, o).wait_recv()
    remote(sm.at[o], em.at[o, pl.ds(leaves, leaves)], m_send.at[2, o], m_recv.at[1, o], d, o).wait_recv()
    remote(sn.at[o], en.at[o, 1], n_send.at[2, o], n_recv.at[1, o], d, o).wait_recv()
    get_lcp.wait()
    get_ncp.wait()
    get_tcp.wait()
    first = jnp.full((cols, 128), c, jnp.int32) == 0

    def keep(i, both):
        a, b = both[:cols], both[cols:]
        ox[i] = jnp.where(first, a, b)
        sx[i] = jnp.where(first, b, a)

    for l in range(leaves):
        keep(l, coupled(lambda s, i: em[s, i], lambda j: source(leaf_ref[l, j], leaves, 24), lcp[l]))
    keep(leaves, coupled(lambda s, i: en[s, i], lambda j: source(node_ref[0, j], 1, 3), ncp[0]))
    send(sx, rx, x_send.at[0], x_recv.at[0], d, o)

    lax.fori_loop(3, 8, near, 0)

    for k in range(1, 16):
        remote(st, tb.at[g], t_send.at[k], t_recv.at[k], d, o).wait_recv()

    def top_index(j):
        v = top_ref[g, j]
        return jnp.where(v >= 0, v, 16)

    both = coupled(lambda s, i: tb[i, s], top_index, tcp[...])
    a, b = both[:cols], both[cols:]
    sp[...] = jnp.where(first, b, a)
    send(sp, rp, x_send.at[1], x_recv.at[1], d, o)
    remote(sx, rx, x_send.at[0], x_recv.at[0], d, o).wait_recv()
    remote(sp, rp, x_send.at[1], x_recv.at[1], d, o).wait_recv()
    top_local = jnp.where(first, a, b) + rp[...]
    node_local = ox[leaves] + rx[leaves] + dot3(stacked(top_local), nth[...], ntl[...], NT)
    node2 = stacked(node_local)
    for l in range(leaves):
        leaf_local = ox[l] + rx[l] + dot3(node2, lth[l], ltl[l], NT)
        far = dot3(stacked(leaf_local), bh[l], bl[l], NT)
        out[:, l * 256 : (l + 1) * 256] = out[:, l * 256 : (l + 1) * 256] + far
    for copy in sends:
        copy.wait_send()


def body(
    coords, values, leaf_basis, leaf_transfer, node_transfer, leaf_coupling, node_coupling, top_coupling,
    near_list, leaf_list, node_list, top_list,
):
    cols = values.shape[0]
    any_ref = pl.BlockSpec(memory_space=pl.ANY)
    smem = pl.BlockSpec(memory_space=pltpu.SMEM)
    vmem = pl.BlockSpec(memory_space=pltpu.VMEM)
    dma = pltpu.SemaphoreType.DMA
    return pl.pallas_call(
        kernel,
        out_shape=jax.ShapeDtypeStruct(values.shape, F32),
        in_specs=[smem] * 4 + [vmem] + [any_ref] * 7,
        out_specs=vmem,
        scratch_shapes=[
            pltpu.VMEM((cols, 2048), F32),
            pltpu.VMEM((2, cols, 2048), F32),
            pltpu.VMEM((25, 8, 128), F32),
            pltpu.VMEM((25, 2 * cols, 256), BF16),
            pltpu.VMEM((3, 256, 128), F32),
            pltpu.VMEM((2, 25, 8, 128), F32),
            pltpu.VMEM((2, 4, 8, 128), F32),
            pltpu.VMEM((8, 2, 8, 128), F32),
            pltpu.VMEM((17, 2, 8, 128), F32),
            pltpu.VMEM((2, 8, 8, 128), F32),
            pltpu.VMEM((2, 8, 128), F32),
            pltpu.VMEM((2, 8, 128), F32),
            pltpu.VMEM((2, 8, 128), F32),
            pltpu.VMEM((8, 256, 128), F32),
            pltpu.VMEM((8, 128, 128), F32),
            pltpu.VMEM((1, 128, 128), F32),
            pltpu.VMEM((8, 8, 64, 128), F32),
            pltpu.VMEM((1, 2, 64, 128), F32),
            pltpu.VMEM((4, 64, 128), F32),
            pltpu.VMEM((8, 256, 128), BF16),
            pltpu.VMEM((8, 256, 128), BF16),
            pltpu.VMEM((8, 128, 128), BF16),
            pltpu.VMEM((8, 128, 128), BF16),
            pltpu.VMEM((128, 128), BF16),
            pltpu.VMEM((128, 128), BF16),
            pltpu.VMEM((9, cols, 128), F32),
            pltpu.VMEM((9, cols, 128), F32),
            pltpu.VMEM((9, cols, 128), F32),
            pltpu.VMEM((cols, 128), F32),
            pltpu.VMEM((cols, 128), F32),
            dma((7,)),
            dma((2,)), dma((2,)), dma((2,)), dma((2,)),
            dma((3, 2)), dma((3, 2)), dma((3, 2)), dma((3, 2)),
            dma((8, 2)), dma((8, 2)), dma((16,)), dma((16,)),
            dma((2,)), dma((2,)),
        ],
        compiler_params=pltpu.CompilerParams(collective_id=0, has_side_effects=True),
    )(
        near_list, leaf_list, node_list, top_list, coords, values,
        leaf_basis, leaf_transfer, node_transfer, leaf_coupling, node_coupling, top_coupling,
    )


def solution(mesh):
    in_specs = (
        P(None, "leaf"),
        P("col", "leaf"),
        P("leaf", None, None),
        P("leaf", None, None),
        P("leaf", None, None),
        P("leaf", None, "col", None),
        P("leaf", None, "col", None),
        P(None, None, "col", None),
        P("leaf", None),
        P("leaf", None),
        P("leaf", None),
        P(),
    )
    return jax.shard_map(body, mesh=mesh, in_specs=in_specs, out_specs=P("col", "leaf"), check_vma=False)
```

time: 209 us -> 38.2 us (0.18)
  waiting for transfers between devices: 84.5 us -> 0 us
  Pallas kernels: 0 us -> 35 us
  matrix products: 30 us -> 0 us
  other arithmetic: 28.5 us -> 0 us
  starting transfers between devices: 17 us -> 0 us
  between operations: 15.8 us -> 0.01 us
  local copies, waits for them, and re-layouts: 17.6 us -> 2.92 us
  blocking collectives: 14.3 us -> 0 us
    all_gather x1 -> x0, waiting for transfers between devices: 84.4 us -> none  [body(): everything = lax.all_gather(contrib, 'leaf', axis=0, tiled=True)]
    pallas_call x0 -> x1, Pallas kernels: none -> 35 us  [body(): pl.pallas_call(kernel, out_shape=jax.ShapeDtypeStruct(values.shape, F32),...]
    dot_general x17 -> x0, matrix products: 30 us -> none  [the longest x8 17.4 us: body(): term = jnp.einsum('lab,clb->lca', kernel, source_rows[3:], precision=high)]
    ppermute x6 -> x0, starting transfers between devices: 16.9 us -> none  [the longest x3 13 us: extended_2(): before = lax.ppermute(last, axis, up)]
    all_gather x3 -> x0, blocking collectives: 14.3 us -> none  [couple(): wide_moments = lax.all_gather(sources, 'col', axis=1, tiled=True)]
    reduce_sum x2 -> x0, other arithmetic: 12.3 us -> none  [the longest x1 11 us: body(): jnp.sum((target[:, :, :, None] - source_rows[:3, :, None, :]) ** 2, axis=0)]
    gather x11 -> x0, local copies, waits for them, and re-layouts: 8.38 us -> none  [the longest x8 5.88 us: body(): source_rows = jnp.take(extended, jnp.maximum(column, 0), axis=1)]
    slice x16 -> x0, local copies, waits for them, and re-layouts: 4.28 us -> none  [body(): source_rows[:3, :, None, :]]
  transfers between devices with their start and end apart: 10 -> 0, of which waited for: 2 -> 0; matrix products, arithmetic and copies ran while one was open for 31% -> 0% of each run, Pallas kernels for 0% -> 0%
where the time goes in v1:
time: 38.2 us; the launch traced here: 38 us
  Pallas kernels  35 us (92%)
  local copies, waits for them, and re-layouts  2.92 us (8%)
    pallas_call x1, Pallas kernels, body(): pl.pallas_call(kernel, out_shape=jax.ShapeDtypeStruct(values.shape, F32),...  35 us
    unnamed x2, local copies, waits for them, and re-layouts  2.92 us

profile of v1, /device:TPU:1, one launch (start us, length us, event | category | flops | bytes accessed | tf_op | source)
XLA Modules:
  0.0 38.0 jit_solution(1375303787359425928)
XLA Ops:
  0.0 1.4 %copy.13.top_ref = s32[16,4]{1,0:T(8,128)} copy(s32[16,4]{0,1:T(4,128)} %param.23) | data formatting | bytes 512 | tf_op args[11]
  1.4 35.0 %shard_map.118 = f32[16,2048]{1,0:T(8,128)} custom-call(s32[8,8]{1,0:T(8,128)} %near_ref.1, s32[8,8]{1,0:T(8,128)} %leaf_ref.1, s32[1,2]{1,0:T(1,128)} %node_ref.1, s32[16,4]{1,0:T(8,128)} %copy.13.top_ref, f32[3,2048]{1,0:T(4,128)} %coords.1, f32[16,2048]{1,0:T(8,128)} %values_hbm.1, f32[8,256,128]{2,1,0:T(8,128)} %basis_hbm.1, f32[8,128,128]{2,1,0:T(8,128)} %ltr_hbm.1, ...), custom_call_target="tpu_custom_call" | custom-call | tf_op jit(solution)/shard_map/pallas_call | solution.py:271
  36.4 1.6 %copy.15 = f32[16,2048]{1,0:T(8,128)} copy(f32[16,2048]{1,0:T(8,128)} %shard_map.118) | data formatting | bytes 262144

commit v2 on v1

v2 whole, which is shorter than its diff:
```python
import functools

import jax
import jax.numpy as jnp
from jax import lax
from jax.experimental import pallas as pl
from jax.experimental.pallas import tpu as pltpu
from jax.sharding import PartitionSpec as P

SOFTENING = 0.01
F32, BF16 = jnp.float32, jnp.bfloat16
MESH = pl.DeviceIdType.MESH
NN = (((1,), (0,)), ((), ()))
NT = (((1,), (1,)), ((), ()))


def mm(a, b, dims):
    return lax.dot_general(a, b, dims, preferred_element_type=F32)


def split(x):
    hi = x.astype(BF16)
    return hi, (x - hi.astype(F32)).astype(BF16)


def stacked(x):
    return jnp.concatenate(split(x), axis=0)


def dot3(x2, yh, yl, dims):
    m = x2.shape[0] // 2
    both = mm(x2, yh, dims)
    return both[:m] + both[m:] + mm(x2[:m], yl, dims)


def kernel(
    near_hbm, leaf_hbm, node_hbm, top_hbm, coords_hbm,
    values_hbm, basis_hbm, ltr_hbm, ntr_hbm, lcp_hbm, ncp_hbm, tcp_hbm,
    out,
    near_ref, leaf_ref, node_ref, top_ref, coords,
    vals, ev, cs, vs, bx, em, en, zb, tb, sm, sn, sc, st,
    basis, ltr, ntr, lcp, ncp, tcp, bh, bl, lth, ltl, nth, ntl, tth, ttl,
    ox, sx, rx,
    local_sem, v_send, v_recv, c_send, c_recv, m_send, m_recv, n_send, n_recv,
    z_send, z_recv, t_send, t_recv, x_send, x_recv,
):
    leaves, chips = 8, 128
    cols = vals.shape[0]
    d, c = lax.axis_index("leaf"), lax.axis_index("col")
    o = 1 - c
    z, g = lax.rem(d, 8), lax.div(d, 8)
    after, before = lax.rem(d + 1, chips), lax.rem(d + chips - 1, chips)

    def fetch(i, src, dst):
        copy = pltpu.make_async_copy(src, dst, local_sem.at[i])
        copy.start()
        return copy

    get_values = fetch(0, values_hbm, vals)
    quarters = [pl.ds(4 * i, 4) for i in range(2)]
    get_basis = [fetch(1 + i, basis_hbm.at[q], basis.at[q]) for i, q in enumerate(quarters)]
    get_ltr = fetch(3, ltr_hbm, ltr)
    get_ntr = fetch(4, ntr_hbm, ntr)
    get_coords = fetch(5, coords_hbm, coords)
    get_tcp = fetch(6, tcp_hbm.at[g], tcp.at[c])
    get_lists = [
        fetch(7 + i, src, dst)
        for i, (src, dst) in enumerate(
            ((near_hbm, near_ref), (leaf_hbm, leaf_ref), (node_hbm, node_ref), (top_hbm, top_ref))
        )
    ]
    get_lcp = fetch(11, lcp_hbm, lcp)
    get_ncp = fetch(12, ncp_hbm, ncp)

    barrier = pltpu.get_barrier_semaphore()

    def greet(leaf, col):
        pl.semaphore_signal(barrier, inc=1, device_id=(leaf, col), device_id_type=MESH)

    for k in range(1, 8):
        greet(g * 8 + lax.rem(z + k, 8), c)
    for h in range(2):
        greet(after, h)
        greet(before, h)
    greet(d, o)
    for k in range(1, 16):
        greet(lax.rem(g + k, 16) * 8 + z, c)

    def remote(src, dst, ssem, rsem, leaf, col):
        return pltpu.make_async_remote_copy(
            src_ref=src, dst_ref=dst, send_sem=ssem, recv_sem=rsem,
            device_id=(leaf, col), device_id_type=MESH,
        )

    sends = []

    def send(*args):
        copy = remote(*args)
        copy.start()
        sends.append(copy)

    get_values.wait()
    for l in range(leaves):
        vs[leaves + l] = stacked(vals[:, l * 256 : (l + 1) * 256])
    moments = []
    for l in range(leaves):
        if l % 4 == 0:
            get_basis[l // 4].wait()
        hi, lo = split(basis[l])
        bh[l], bl[l] = hi, lo
        moments.append(dot3(vs[leaves + l], hi, lo, NN))
    get_ltr.wait()
    lth[...], ltl[...] = split(ltr[...])
    down = (leaves * 128, 128)
    node = dot3(stacked(jnp.concatenate(moments, 1)), lth[...].reshape(down), ltl[...].reshape(down), NN)
    get_ntr.wait()
    nth[...], ntl[...] = split(ntr[0])
    contrib = dot3(stacked(node), nth[...], ntl[...], NN)
    sc[...] = contrib
    pl.semaphore_wait(barrier, 27)
    for k in range(1, 8):
        send(sc, zb.at[k], z_send.at[k], z_recv.at[k], g * 8 + lax.rem(z + k, 8), c)

    low = lax.broadcasted_iota(jnp.int32, (8, 128), 1) < 64

    def half(x, h):
        a, b = x[:8], x[8:]
        return jnp.where(low, a, pltpu.roll(b, 64, 1)) if h == 0 else jnp.where(low, pltpu.roll(a, 64, 1), b)

    for h in range(2):
        sn[h] = half(node, h)
        for l in range(leaves):
            sm[h, l] = half(moments[l], h)
    own = pl.ds(leaves, leaves)
    get_tcp.wait()
    send(tcp.at[c], tcp.at[c], x_send.at[1], x_recv.at[1], d, o)
    send(sm.at[o], em.at[c, own], m_send.at[2, o], m_recv.at[1, c], d, o)
    send(sn.at[o], en.at[c, 1], n_send.at[2, o], n_recv.at[1, c], d, o)
    for q, leaf in ((0, after), (1, before)):
        for h in range(2):
            send(sn.at[h], en.at[c, 2 * q], n_send.at[q, h], n_recv.at[2 * q, c], leaf, h)
            send(sm.at[h], em.at[c, pl.ds(16 * q, leaves)], m_send.at[q, h], m_recv.at[2 * q, c], leaf, h)
    em[c, own] = sm[c]
    en[c, 1] = sn[c]

    zero8 = jnp.zeros((8, 128), F32)
    get_coords.wait()
    for l in range(leaves):
        for h in range(2):
            start = l * 256 + h * 128
            cs[leaves + l, 3 * h : 3 * h + 3, :] = coords[:, start : start + 128]
        cs[leaves + l, 6:8, :] = zero8[:2]
    for q, leaf in ((0, after), (1, before)):
        send(vals, ev.at[q], v_send.at[q], v_recv.at[q], leaf, c)
        send(cs.at[own], cs.at[pl.ds(16 * q, leaves)], c_send.at[q], c_recv.at[q], leaf, c)
    cs[24] = zero8
    vs[24] = jnp.zeros((2 * cols, 256), BF16)
    tb[16] = jnp.zeros((cols, 128), F32)
    for s in range(2):
        em[s, 24] = zero8
        en[s, 3] = zero8

    total = contrib
    for k in range(1, 8):
        remote(sc, zb.at[k], z_send.at[k], z_recv.at[k], d, o).wait_recv()
    for k in range(1, 8):
        total = total + zb[k]
    st[...] = total
    for k in range(1, 16):
        send(st, tb.at[g], t_send.at[k], t_recv.at[k], lax.rem(g + k, 16) * 8 + z, c)
    tb[g] = total

    def source(v, first, none):
        return jnp.where(v >= 0, jnp.clip(v - first, 0, none - 1), none)

    def paired(load, i, j):
        rows = []
        for s in range(2):
            a, b = load(s, i), load(s, j)
            rows += [jnp.where(low, a, pltpu.roll(b, 64, 1)), jnp.where(low, pltpu.roll(a, 64, 1), b)]
        return jnp.concatenate(rows, 0)

    def coupled(load, index, blocks):
        slots = blocks.shape[0]
        picked = jnp.concatenate([paired(load, index(j), index(j + 1)) for j in range(0, slots, 2)], 1)
        return dot3(stacked(picked), *split(blocks.reshape(slots * 64, 128)), NN)

    for h in range(2):
        for q in (0, 2):
            remote(sm.at[h], em.at[h, pl.ds(8 * q, leaves)], m_send.at[0, h], m_recv.at[q, h], d, o).wait_recv()
            remote(sn.at[h], en.at[h, q], n_send.at[0, h], n_recv.at[q, h], d, o).wait_recv()
    remote(sm.at[o], em.at[o, own], m_send.at[2, o], m_recv.at[1, o], d, o).wait_recv()
    remote(sn.at[o], en.at[o, 1], n_send.at[2, o], n_recv.at[1, o], d, o).wait_recv()
    for copy in (*get_lists, get_lcp, get_ncp):
        copy.wait()
    first = jnp.full((cols, 128), c, jnp.int32) == 0

    def keep(i, both):
        a, b = both[:cols], both[cols:]
        ox[i] = jnp.where(first, a, b)
        sx[i] = jnp.where(first, b, a)

    for l in range(leaves):
        keep(l, coupled(lambda s, i: em[s, i], lambda j: source(leaf_ref[l, j], (d - 1) * leaves, 24), lcp[l]))
    keep(leaves, coupled(lambda s, i: en[s, i], lambda j: source(node_ref[0, j], d - 1, 3), ncp[0]))
    send(sx, rx, x_send.at[0], x_recv.at[0], d, o)
    remote(tcp.at[o], tcp.at[o], x_send.at[1], x_recv.at[1], d, o).wait_recv()
    for j in range(4):
        for h in range(2):
            rows = pl.ds(j * 128 + h * 64, 64)
            tth[rows], ttl[rows] = split(tcp[h, j])

    for q in range(2):
        remote(vals, ev.at[q], v_send.at[q], v_recv.at[q], after, c).wait_recv()
        mine = cs.at[pl.ds(16 * q, leaves)]
        remote(mine, mine, c_send.at[q], c_recv.at[q], after, c).wait_recv()
        for l in range(leaves):
            vs[16 * q + l] = stacked(ev[q, :, l * 256 : (l + 1) * 256])

    def near(l, carry):
        points = cs[leaves + l].T
        for k in range(3):
            bx[k, 0:128, :] = jnp.broadcast_to(points[:, k : k + 1], (128, 128))
            bx[k, 128:256, :] = jnp.broadcast_to(points[:, 3 + k : 4 + k], (128, 128))
        total = None
        for j in range(8):
            i = source(near_ref[l, j], (d - 1) * leaves, 24)
            rows = cs[i]
            his, los = [], []
            for h in range(2):
                r2 = None
                for k in range(3):
                    e = bx[k] - rows[3 * h + k : 3 * h + k + 1, :]
                    r2 = e * e if r2 is None else r2 + e * e
                hi, lo = split(lax.rsqrt(r2 + SOFTENING))
                his.append(hi)
                los.append(lo)
            term = dot3(vs[i], jnp.concatenate(his, 1), jnp.concatenate(los, 1), NT)
            total = term if total is None else total + term
        out[:, pl.ds(pl.multiple_of(l * 256, 256), 256)] = total * (1.0 / 16.0)
        return carry

    lax.fori_loop(0, 8, near, 0)

    remote(sx, rx, x_send.at[0], x_recv.at[0], d, o).wait_recv()
    for k in range(1, 16):
        remote(st, tb.at[g], t_send.at[k], t_recv.at[k], d, o).wait_recv()
    picked = jnp.concatenate([tb[source(top_ref[j, g], 0, 16)] for j in range(4)], 1)
    top_local = dot3(stacked(picked), tth[...], ttl[...], NN)
    node_local = ox[leaves] + rx[leaves] + dot3(stacked(top_local), nth[...], ntl[...], NT)
    node2 = stacked(node_local)
    for l in range(leaves):
        leaf_local = ox[l] + rx[l] + dot3(node2, lth[l], ltl[l], NT)
        far = dot3(stacked(leaf_local), bh[l], bl[l], NT)
        out[:, l * 256 : (l + 1) * 256] = out[:, l * 256 : (l + 1) * 256] + far
    for copy in sends:
        copy.wait_send()


def body(
    coords, values, leaf_basis, leaf_transfer, node_transfer, leaf_coupling, node_coupling, top_coupling,
    near_list, leaf_list, node_list, top_list,
):
    cols = values.shape[0]
    any_ref = pl.BlockSpec(memory_space=pl.ANY)
    vmem = pl.BlockSpec(memory_space=pltpu.VMEM)
    dma = pltpu.SemaphoreType.DMA
    return pl.pallas_call(
        kernel,
        out_shape=jax.ShapeDtypeStruct(values.shape, F32),
        in_specs=[any_ref] * 12,
        out_specs=vmem,
        scratch_shapes=[
            pltpu.SMEM((8, 8), jnp.int32),
            pltpu.SMEM((8, 8), jnp.int32),
            pltpu.SMEM((1, 2), jnp.int32),
            pltpu.SMEM((4, 16), jnp.int32),
            pltpu.VMEM((3, 2048), F32),
            pltpu.VMEM((cols, 2048), F32),
            pltpu.VMEM((2, cols, 2048), F32),
            pltpu.VMEM((25, 8, 128), F32),
            pltpu.VMEM((25, 2 * cols, 256), BF16),
            pltpu.VMEM((3, 256, 128), F32),
            pltpu.VMEM((2, 25, 8, 128), F32),
            pltpu.VMEM((2, 4, 8, 128), F32),
            pltpu.VMEM((8, cols, 128), F32),
            pltpu.VMEM((17, cols, 128), F32),
            pltpu.VMEM((2, 8, 8, 128), F32),
            pltpu.VMEM((2, 8, 128), F32),
            pltpu.VMEM((cols, 128), F32),
            pltpu.VMEM((cols, 128), F32),
            pltpu.VMEM((8, 256, 128), F32),
            pltpu.VMEM((8, 128, 128), F32),
            pltpu.VMEM((1, 128, 128), F32),
            pltpu.VMEM((8, 8, 64, 128), F32),
            pltpu.VMEM((1, 2, 64, 128), F32),
            pltpu.VMEM((2, 4, 64, 128), F32),
            pltpu.VMEM((8, 256, 128), BF16),
            pltpu.VMEM((8, 256, 128), BF16),
            pltpu.VMEM((8, 128, 128), BF16),
            pltpu.VMEM((8, 128, 128), BF16),
            pltpu.VMEM((128, 128), BF16),
            pltpu.VMEM((128, 128), BF16),
            pltpu.VMEM((512, 128), BF16),
            pltpu.VMEM((512, 128), BF16),
            pltpu.VMEM((9, cols, 128), F32),
            pltpu.VMEM((9, cols, 128), F32),
            pltpu.VMEM((9, cols, 128), F32),
            dma((13,)),
            dma((2,)), dma((2,)), dma((2,)), dma((2,)),
            dma((3, 2)), dma((3, 2)), dma((3, 2)), dma((3, 2)),
            dma((8,)), dma((8,)), dma((16,)), dma((16,)),
            dma((2,)), dma((2,)),
        ],
        compiler_params=pltpu.CompilerParams(collective_id=0, has_side_effects=True),
    )(
        near_list, leaf_list, node_list, top_list.T, coords, values,
        leaf_basis, leaf_transfer, node_transfer, leaf_coupling, node_coupling, top_coupling,
    )


def solution(mesh):
    in_specs = (
        P(None, "leaf"),
        P("col", "leaf"),
        P("leaf", None, None),
        P("leaf", None, None),
        P("leaf", None, None),
        P("leaf", None, "col", None),
        P("leaf", None, "col", None),
        P(None, None, "col", None),
        P("leaf", None),
        P("leaf", None),
        P("leaf", None),
        P(),
    )
    return jax.shard_map(body, mesh=mesh, in_specs=in_specs, out_specs=P("col", "leaf"), check_vma=False)
```

time: 38.2 us -> 34.5 us (0.903)
  Pallas kernels: 35 us -> 32.8 us
  local copies, waits for them, and re-layouts: 2.92 us -> 1.57 us
    pallas_call x1, Pallas kernels: 35 us -> 32.8 us  [body(): pl.pallas_call(kernel, out_shape=jax.ShapeDtypeStruct(values.shape, F32),...]
    unnamed x2 -> x1, local copies, waits for them, and re-layouts: 2.92 us -> 1.57 us
where the time goes in v2:
time: 34.5 us; the launch traced here: 34.4 us
  Pallas kernels  32.8 us (95%)
  local copies, waits for them, and re-layouts  1.57 us (5%)
    pallas_call x1, Pallas kernels, body(): pl.pallas_call(kernel, out_shape=jax.ShapeDtypeStruct(values.shape, F32),...  32.8 us
    unnamed x1, local copies, waits for them, and re-layouts  1.57 us

profile of v2, /device:TPU:1, one launch (start us, length us, event | category | flops | bytes accessed | tf_op | source)
XLA Modules:
  0.0 34.4 jit_solution(2089286954741023422)
XLA Ops:
  0.0 32.8 %shard_map.118 = f32[16,2048]{1,0:T(8,128)} custom-call(s32[8,8]{1,0:T(8,128)} %near_hbm.1, s32[8,8]{1,0:T(8,128)} %leaf_hbm.1, s32[1,2]{1,0:T(1,128)} %node_hbm.1, s32[4,16]{1,0:T(4,128)} %bitcast.1, f32[3,2048]{1,0:T(4,128)} %coords_hbm.1, f32[16,2048]{1,0:T(8,128)} %values_hbm.1, f32[8,256,128]{2,1,0:T(8,128)} %basis_hbm.1, f32[8,128,128]{2,1,0:T(8,128)} %ltr_hbm.1, ...), custom_call_target="tpu_custom_call" | custom-call | tf_op jit(solution)/shard_map/pallas_call | solution.py:268
  32.8 1.6 %copy.14 = f32[16,2048]{1,0:T(8,128)} copy(f32[16,2048]{1,0:T(8,128)} %shard_map.118) | data formatting | bytes 262144

commit v3 on v2

--- a/solution.py
+++ b/solution.py
@@ -8,6 +8,7 @@
 from jax.sharding import PartitionSpec as P
 
 SOFTENING = 0.01
+AHEAD = 3
 F32, BF16 = jnp.float32, jnp.bfloat16
 MESH = pl.DeviceIdType.MESH
 NN = (((1,), (0,)), ((), ()))
@@ -42,7 +43,7 @@
     basis, ltr, ntr, lcp, ncp, tcp, bh, bl, lth, ltl, nth, ntl, tth, ttl,
     ox, sx, rx,
     local_sem, v_send, v_recv, c_send, c_recv, m_send, m_recv, n_send, n_recv,
-    z_send, z_recv, t_send, t_recv, x_send, x_recv,
+    z_send, z_recv, t_send, t_recv, x_send, x_recv, tokens,
 ):
     leaves, chips = 8, 128
     cols = vals.shape[0]
@@ -77,14 +78,32 @@
     def greet(leaf, col):
         pl.semaphore_signal(barrier, inc=1, device_id=(leaf, col), device_id_type=MESH)
 
-    for k in range(1, 8):
-        greet(g * 8 + lax.rem(z + k, 8), c)
-    for h in range(2):
-        greet(after, h)
-        greet(before, h)
+    def chip(x, y, z):
+        return (lax.rem(x, 4) * 4 + lax.rem(y, 4)) * 8 + lax.rem(z, 8)
+
+    x, y = lax.div(g, 4), lax.rem(g, 4)
+    x_up, x_down = chip(x + 1, y, z), chip(x + 3, y, z)
+    y_up, y_down = chip(x, y + 1, z), chip(x, y + 3, z)
+    z_up, z_down = chip(x, y, z + 1), chip(x, y, z + 7)
+    no_after, no_before = lax.div(d, chips - 1), lax.div(chips - 1 - d, chips - 1)
+    sides = ((0, after, no_after == 0, no_before == 0), (1, before, no_before == 0, no_after == 0))
+
     greet(d, o)
-    for k in range(1, 16):
-        greet(lax.rem(g + k, 16) * 8 + z, c)
+    for leaf in (z_up, z_down, x_up, x_down, y_up, y_down):
+        greet(leaf, c)
+    for _, leaf, there, _ in sides:
+
+        @pl.when(there)
+        def _(leaf=leaf):
+            greet(leaf, 0)
+            greet(leaf, 1)
+
+    def token(i, leaf):
+        pl.semaphore_signal(tokens.at[i], inc=1, device_id=(leaf, c), device_id_type=MESH)
+
+    def heard(*which):
+        for i in which:
+            pl.semaphore_wait(tokens.at[i], 1)
 
     def remote(src, dst, ssem, rsem, leaf, col):
         return pltpu.make_async_remote_copy(
@@ -99,7 +118,46 @@
         copy.start()
         sends.append(copy)
 
+    own = pl.ds(leaves, leaves)
+    zero8 = jnp.zeros((8, 128), F32)
+
+    def points_to(q, leaf):
+        land = pl.ds(16 * q, leaves)
+        return (
+            remote(vals, ev.at[q], v_send.at[q], v_recv.at[q], leaf, c),
+            remote(cs.at[own], cs.at[land], c_send.at[q], c_recv.at[q], leaf, c),
+        )
+
+    def moments_to(q, leaf):
+        land = pl.ds(16 * q, leaves)
+        return [
+            copy
+            for h in range(2)
+            for copy in (
+                remote(sn.at[h], en.at[c, 2 * q], n_send.at[q, h], n_recv.at[2 * q, c], leaf, h),
+                remote(sm.at[h], em.at[c, land], m_send.at[q, h], m_recv.at[2 * q, c], leaf, h),
+            )
+        ]
+
+    get_coords.wait()
+    for l in range(leaves):
+        for h in range(2):
+            start = l * 256 + h * 128
+            cs[leaves + l, 3 * h : 3 * h + 3, :] = coords[:, start : start + 128]
+        cs[leaves + l, 6:8, :] = zero8[:2]
     get_values.wait()
+    pl.semaphore_wait(barrier, 11 - 2 * no_after - 2 * no_before)
+    for q, leaf, there, _ in sides:
+
+        @pl.when(there)
+        def _(q=q, leaf=leaf):
+            for copy in points_to(q, leaf):
+                copy.start()
+
+    token(0, z_up)
+    token(3, z_down)
+    token(5, x_down)
+
     for l in range(leaves):
         vs[leaves + l] = stacked(vals[:, l * 256 : (l + 1) * 256])
     moments = []
@@ -117,7 +175,16 @@
     nth[...], ntl[...] = split(ntr[0])
     contrib = dot3(stacked(node), nth[...], ntl[...], NN)
     sc[...] = contrib
-    pl.semaphore_wait(barrier, 27)
+    heard(0)
+    token(1, z_up)
+    heard(3)
+    token(4, z_down)
+    heard(5)
+    token(6, y_up)
+    token(8, y_down)
+    heard(1)
+    token(2, z_up)
+    heard(4, 2)
     for k in range(1, 8):
         send(sc, zb.at[k], z_send.at[k], z_recv.at[k], g * 8 + lax.rem(z + k, 8), c)
 
@@ -131,28 +198,22 @@
         sn[h] = half(node, h)
         for l in range(leaves):
             sm[h, l] = half(moments[l], h)
-    own = pl.ds(leaves, leaves)
     get_tcp.wait()
     send(tcp.at[c], tcp.at[c], x_send.at[1], x_recv.at[1], d, o)
     send(sm.at[o], em.at[c, own], m_send.at[2, o], m_recv.at[1, c], d, o)
     send(sn.at[o], en.at[c, 1], n_send.at[2, o], n_recv.at[1, c], d, o)
-    for q, leaf in ((0, after), (1, before)):
-        for h in range(2):
-            send(sn.at[h], en.at[c, 2 * q], n_send.at[q, h], n_recv.at[2 * q, c], leaf, h)
-            send(sm.at[h], em.at[c, pl.ds(16 * q, leaves)], m_send.at[q, h], m_recv.at[2 * q, c], leaf, h)
+    for q, leaf, there, _ in sides:
+
+        @pl.when(there)
+        def _(q=q, leaf=leaf):
+            for copy in moments_to(q, leaf):
+                copy.start()
+
     em[c, own] = sm[c]
     en[c, 1] = sn[c]
 
-    zero8 = jnp.zeros((8, 128), F32)
-    get_coords.wait()
-    for l in range(leaves):
-        for h in range(2):
-            start = l * 256 + h * 128
-            cs[leaves + l, 3 * h : 3 * h + 3, :] = coords[:, start : start + 128]
-        cs[leaves + l, 6:8, :] = zero8[:2]
-    for q, leaf in ((0, after), (1, before)):
-        send(vals, ev.at[q], v_send.at[q], v_recv.at[q], leaf, c)
-        send(cs.at[own], cs.at[pl.ds(16 * q, leaves)], c_send.at[q], c_recv.at[q], leaf, c)
+    heard(6)
+    token(7, y_up)
     cs[24] = zero8
     vs[24] = jnp.zeros((2 * cols, 256), BF16)
     tb[16] = jnp.zeros((cols, 128), F32)
@@ -160,62 +221,18 @@
         em[s, 24] = zero8
         en[s, 3] = zero8
 
-    total = contrib
-    for k in range(1, 8):
-        remote(sc, zb.at[k], z_send.at[k], z_recv.at[k], d, o).wait_recv()
-    for k in range(1, 8):
-        total = total + zb[k]
-    st[...] = total
-    for k in range(1, 16):
-        send(st, tb.at[g], t_send.at[k], t_recv.at[k], lax.rem(g + k, 16) * 8 + z, c)
-    tb[g] = total
-
     def source(v, first, none):
         return jnp.where(v >= 0, jnp.clip(v - first, 0, none - 1), none)
 
-    def paired(load, i, j):
-        rows = []
-        for s in range(2):
-            a, b = load(s, i), load(s, j)
-            rows += [jnp.where(low, a, pltpu.roll(b, 64, 1)), jnp.where(low, pltpu.roll(a, 64, 1), b)]
-        return jnp.concatenate(rows, 0)
-
-    def coupled(load, index, blocks):
-        slots = blocks.shape[0]
-        picked = jnp.concatenate([paired(load, index(j), index(j + 1)) for j in range(0, slots, 2)], 1)
-        return dot3(stacked(picked), *split(blocks.reshape(slots * 64, 128)), NN)
-
-    for h in range(2):
-        for q in (0, 2):
-            remote(sm.at[h], em.at[h, pl.ds(8 * q, leaves)], m_send.at[0, h], m_recv.at[q, h], d, o).wait_recv()
-            remote(sn.at[h], en.at[h, q], n_send.at[0, h], n_recv.at[q, h], d, o).wait_recv()
-    remote(sm.at[o], em.at[o, own], m_send.at[2, o], m_recv.at[1, o], d, o).wait_recv()
-    remote(sn.at[o], en.at[o, 1], n_send.at[2, o], n_recv.at[1, o], d, o).wait_recv()
-    for copy in (*get_lists, get_lcp, get_ncp):
-        copy.wait()
-    first = jnp.full((cols, 128), c, jnp.int32) == 0
-
-    def keep(i, both):
-        a, b = both[:cols], both[cols:]
-        ox[i] = jnp.where(first, a, b)
-        sx[i] = jnp.where(first, b, a)
-
-    for l in range(leaves):
-        keep(l, coupled(lambda s, i: em[s, i], lambda j: source(leaf_ref[l, j], (d - 1) * leaves, 24), lcp[l]))
-    keep(leaves, coupled(lambda s, i: en[s, i], lambda j: source(node_ref[0, j], d - 1, 3), ncp[0]))
-    send(sx, rx, x_send.at[0], x_recv.at[0], d, o)
-    remote(tcp.at[o], tcp.at[o], x_send.at[1], x_recv.at[1], d, o).wait_recv()
-    for j in range(4):
-        for h in range(2):
-            rows = pl.ds(j * 128 + h * 64, 64)
-            tth[rows], ttl[rows] = split(tcp[h, j])
-
-    for q in range(2):
-        remote(vals, ev.at[q], v_send.at[q], v_recv.at[q], after, c).wait_recv()
-        mine = cs.at[pl.ds(16 * q, leaves)]
-        remote(mine, mine, c_send.at[q], c_recv.at[q], after, c).wait_recv()
-        for l in range(leaves):
-            vs[16 * q + l] = stacked(ev[q, :, l * 256 : (l + 1) * 256])
+    def take_points():
+        for q, leaf, _, there in sides:
+
+            @pl.when(there)
+            def _(q=q, leaf=leaf):
+                for copy in points_to(q, leaf):
+                    copy.wait_recv()
+                for l in range(leaves):
+                    vs[16 * q + l] = stacked(ev[q, :, l * 256 : (l + 1) * 256])
 
     def near(l, carry):
         points = cs[leaves + l].T
@@ -240,7 +257,74 @@
         out[:, pl.ds(pl.multiple_of(l * 256, 256), 256)] = total * (1.0 / 16.0)
         return carry
 
-    lax.fori_loop(0, 8, near, 0)
+    for copy in get_lists:
+        copy.wait()
+    ahead = jnp.where(z < 4, AHEAD, 0)
+
+    @pl.when(z < 4)
+    def _():
+        take_points()
+
+    lax.fori_loop(0, ahead, near, 0)
+
+    total = contrib
+    for k in range(1, 8):
+        remote(sc, zb.at[k], z_send.at[k], z_recv.at[k], d, o).wait_recv()
+    for k in range(1, 8):
+        total = total + zb[k]
+    st[...] = total
+    heard(8, 7)
+    for k in range(1, 16):
+        send(st, tb.at[g], t_send.at[k], t_recv.at[k], lax.rem(g + k, 16) * 8 + z, c)
+    tb[g] = total
+
+    def paired(load, i, j):
+        rows = []
+        for s in range(2):
+            a, b = load(s, i), load(s, j)
+            rows += [jnp.where(low, a, pltpu.roll(b, 64, 1)), jnp.where(low, pltpu.roll(a, 64, 1), b)]
+        return jnp.concatenate(rows, 0)
+
+    def coupled(load, index, blocks):
+        slots = blocks.shape[0]
+        picked = jnp.concatenate([paired(load, index(j), index(j + 1)) for j in range(0, slots, 2)], 1)
+        return dot3(stacked(picked), *split(blocks.reshape(slots * 64, 128)), NN)
+
+    for q, _, _, there in sides:
+
+        @pl.when(there)
+        def _(q=q):
+            for h in range(2):
+                land = pl.ds(16 * q, leaves)
+                remote(sm.at[h], em.at[h, land], m_send.at[0, h], m_recv.at[2 * q, h], d, o).wait_recv()
+                remote(sn.at[h], en.at[h, 2 * q], n_send.at[0, h], n_recv.at[2 * q, h], d, o).wait_recv()
+
+    remote(sm.at[o], em.at[o, own], m_send.at[2, o], m_recv.at[1, o], d, o).wait_recv()
+    remote(sn.at[o], en.at[o, 1], n_send.at[2, o], n_recv.at[1, o], d, o).wait_recv()
+    for copy in (get_lcp, get_ncp):
+        copy.wait()
+    first = jnp.full((cols, 128), c, jnp.int32) == 0
+
+    def keep(i, both):
+        a, b = both[:cols], both[cols:]
+        ox[i] = jnp.where(first, a, b)
+        sx[i] = jnp.where(first, b, a)
+
+    for l in range(leaves):
+        keep(l, coupled(lambda s, i: em[s, i], lambda j: source(leaf_ref[l, j], (d - 1) * leaves, 24), lcp[l]))
+    keep(leaves, coupled(lambda s, i: en[s, i], lambda j: source(node_ref[0, j], d - 1, 3), ncp[0]))
+    send(sx, rx, x_send.at[0], x_recv.at[0], d, o)
+    remote(tcp.at[o], tcp.at[o], x_send.at[1], x_recv.at[1], d, o).wait_recv()
+    for j in range(4):
+        for h in range(2):
+            rows = pl.ds(j * 128 + h * 64, 64)
+            tth[rows], ttl[rows] = split(tcp[h, j])
+
+    @pl.when(z >= 4)
+    def _():
+        take_points()
+
+    lax.fori_loop(ahead, 8, near, 0)
 
     remote(sx, rx, x_send.at[0], x_recv.at[0], d, o).wait_recv()
     for k in range(1, 16):
@@ -255,6 +339,12 @@
         out[:, l * 256 : (l + 1) * 256] = out[:, l * 256 : (l + 1) * 256] + far
     for copy in sends:
         copy.wait_send()
+    for q, leaf, there, _ in sides:
+
+        @pl.when(there)
+        def _(q=q, leaf=leaf):
+            for copy in (*points_to(q, leaf), *moments_to(q, leaf)):
+                copy.wait_send()
 
 
 def body(
@@ -310,7 +400,7 @@
             dma((2,)), dma((2,)), dma((2,)), dma((2,)),
             dma((3, 2)), dma((3, 2)), dma((3, 2)), dma((3, 2)),
             dma((8,)), dma((8,)), dma((16,)), dma((16,)),
-            dma((2,)), dma((2,)),
+            dma((2,)), dma((2,)), pltpu.SemaphoreType.REGULAR((9,)),
         ],
         compiler_params=pltpu.CompilerParams(collective_id=0, has_side_effects=True),
     )(

time: 34.5 us -> 31.4 us (0.910)
  the two profiles are of different devices: /device:TPU:1 before, /device:TPU:2 now
where the time goes in v3:
time: 31.4 us; the launch traced here: 31.3 us
  Pallas kernels  29.7 us (95%)
  local copies, waits for them, and re-layouts  1.57 us (5%)
    pallas_call x1, Pallas kernels, body(): pl.pallas_call(kernel, out_shape=jax.ShapeDtypeStruct(values.shape, F32),...  29.7 us
    unnamed x1, local copies, waits for them, and re-layouts  1.57 us

profile of v3, /device:TPU:2, one launch (start us, length us, event | category | flops | bytes accessed | tf_op | source)
XLA Modules:
  0.0 31.3 jit_solution(14163189545096641349)
XLA Ops:
  0.0 29.7 %shard_map.118 = f32[16,2048]{1,0:T(8,128)} custom-call(s32[8,8]{1,0:T(8,128)} %near_hbm.1, s32[8,8]{1,0:T(8,128)} %leaf_hbm.1, s32[1,2]{1,0:T(1,128)} %node_hbm.1, s32[4,16]{1,0:T(4,128)} %bitcast.1, f32[3,2048]{1,0:T(4,128)} %coords_hbm.1, f32[16,2048]{1,0:T(8,128)} %values_hbm.1, f32[8,256,128]{2,1,0:T(8,128)} %basis_hbm.1, f32[8,128,128]{2,1,0:T(8,128)} %ltr_hbm.1, ...), custom_call_target="tpu_custom_call" | custom-call | tf_op jit(solution)/shard_map/pallas_call | solution.py:358
  29.7 1.6 %copy.14 = f32[16,2048]{1,0:T(8,128)} copy(f32[16,2048]{1,0:T(8,128)} %shard_map.118) | data formatting | bytes 262144

commit v4 on v3

--- a/solution.py
+++ b/solution.py
@@ -8,7 +8,6 @@
 from jax.sharding import PartitionSpec as P
 
 SOFTENING = 0.01
-AHEAD = 3
 F32, BF16 = jnp.float32, jnp.bfloat16
 MESH = pl.DeviceIdType.MESH
 NN = (((1,), (0,)), ((), ()))
@@ -39,11 +38,11 @@
     values_hbm, basis_hbm, ltr_hbm, ntr_hbm, lcp_hbm, ncp_hbm, tcp_hbm,
     out,
     near_ref, leaf_ref, node_ref, top_ref, coords,
-    vals, ev, cs, vs, bx, em, en, zb, tb, sm, sn, sc, st,
+    vals, ev, cs, rv, vs, nk, ns, nr, bx, em, en, zb, tb, sm, sn, sc, st,
     basis, ltr, ntr, lcp, ncp, tcp, bh, bl, lth, ltl, nth, ntl, tth, ttl,
     ox, sx, rx,
     local_sem, v_send, v_recv, c_send, c_recv, m_send, m_recv, n_send, n_recv,
-    z_send, z_recv, t_send, t_recv, x_send, x_recv, tokens,
+    z_send, z_recv, t_send, t_recv, x_send, x_recv, f_send, f_recv, g_send, g_recv, r_send, r_recv, tokens,
 ):
     leaves, chips = 8, 128
     cols = vals.shape[0]
@@ -121,12 +120,13 @@
     own = pl.ds(leaves, leaves)
     zero8 = jnp.zeros((8, 128), F32)
 
-    def points_to(q, leaf):
-        land = pl.ds(16 * q, leaves)
-        return (
-            remote(vals, ev.at[q], v_send.at[q], v_recv.at[q], leaf, c),
-            remote(cs.at[own], cs.at[land], c_send.at[q], c_recv.at[q], leaf, c),
-        )
+    def columns_to(q, leaf, part):
+        rows = pl.ds(part * 8, 8)
+        return remote(vals.at[rows], ev.at[q, rows], v_send.at[q, part], v_recv.at[q, part], leaf, c)
+
+    def coords_to(q, leaf):
+        mine, land = pl.ds(leaves + 4 * c, 4), pl.ds(16 * q + 4 * c, 4)
+        return remote(cs.at[mine], cs.at[land], c_send.at[q], c_recv.at[q], leaf, c)
 
     def moments_to(q, leaf):
         land = pl.ds(16 * q, leaves)
@@ -151,22 +151,24 @@
 
         @pl.when(there)
         def _(q=q, leaf=leaf):
-            for copy in points_to(q, leaf):
-                copy.start()
-
+            coords_to(q, leaf).start()
+            columns_to(q, leaf, 0).start()
+            columns_to(q, leaf, 1).start()
+
+    send(vals, rv.at[2], f_send.at[2], f_recv.at[2], d, o)
     token(0, z_up)
     token(3, z_down)
     token(5, x_down)
 
     for l in range(leaves):
-        vs[leaves + l] = stacked(vals[:, l * 256 : (l + 1) * 256])
+        vs[c, leaves + l] = stacked(vals[:, l * 256 : (l + 1) * 256])
     moments = []
     for l in range(leaves):
         if l % 4 == 0:
             get_basis[l // 4].wait()
         hi, lo = split(basis[l])
         bh[l], bl[l] = hi, lo
-        moments.append(dot3(vs[leaves + l], hi, lo, NN))
+        moments.append(dot3(vs[c, leaves + l], hi, lo, NN))
     get_ltr.wait()
     lth[...], ltl[...] = split(ltr[...])
     down = (leaves * 128, 128)
@@ -215,26 +217,61 @@
     heard(6)
     token(7, y_up)
     cs[24] = zero8
-    vs[24] = jnp.zeros((2 * cols, 256), BF16)
     tb[16] = jnp.zeros((cols, 128), F32)
     for s in range(2):
+        vs[s, 24] = jnp.zeros((2 * cols, 256), BF16)
         em[s, 24] = zero8
         en[s, 3] = zero8
 
     def source(v, first, none):
         return jnp.where(v >= 0, jnp.clip(v - first, 0, none - 1), none)
 
-    def take_points():
+    def forward(q):
+        return remote(ev.at[q], rv.at[q], f_send.at[q], f_recv.at[q], d, o)
+
+    def forward_coords(q, core):
+        land = cs.at[pl.ds(16 * q + 4 * core, 4)]
+        return remote(land, land, g_send.at[q], g_recv.at[q], d, o)
+
+    def pass_on():
         for q, leaf, _, there in sides:
 
             @pl.when(there)
             def _(q=q, leaf=leaf):
-                for copy in points_to(q, leaf):
-                    copy.wait_recv()
+                coords_to(q, leaf).wait_recv()
+                forward_coords(q, c).start()
+                for part in range(2):
+                    columns_to(q, leaf, part).wait_recv()
+                forward(q).start()
+
+    def take_points():
+        for q, _, _, there in sides:
+
+            @pl.when(there)
+            def _(q=q):
                 for l in range(leaves):
-                    vs[16 * q + l] = stacked(ev[q, :, l * 256 : (l + 1) * 256])
-
-    def near(l, carry):
+                    vs[c, 16 * q + l] = stacked(ev[q, :, l * 256 : (l + 1) * 256])
+
+        remote(vals, rv.at[2], f_send.at[2], f_recv.at[2], d, o).wait_recv()
+        for l in range(leaves):
+            vs[o, leaves + l] = stacked(rv[2, :, l * 256 : (l + 1) * 256])
+        for q, _, _, there in sides:
+
+            @pl.when(there)
+            def _(q=q):
+                forward_coords(q, o).wait_recv()
+                forward(q).wait_recv()
+                for l in range(leaves):
+                    vs[o, 16 * q + l] = stacked(rv[q, :, l * 256 : (l + 1) * 256])
+
+    first = jnp.full((cols, 128), c, jnp.int32) == 0
+    wide = jnp.full((cols, 256), c, jnp.int32) == 0
+
+    def result(t):
+        return remote(ns.at[t], nr.at[t], r_send.at[t], r_recv.at[t], d, o)
+
+    def near(t, carry):
+        l = c * 4 + t
         points = cs[leaves + l].T
         for k in range(3):
             bx[k, 0:128, :] = jnp.broadcast_to(points[:, k : k + 1], (128, 128))
@@ -252,21 +289,20 @@
                 hi, lo = split(lax.rsqrt(r2 + SOFTENING))
                 his.append(hi)
                 los.append(lo)
-            term = dot3(vs[i], jnp.concatenate(his, 1), jnp.concatenate(los, 1), NT)
+            v0, v1 = vs[0, i], vs[1, i]
+            v2 = jnp.concatenate([v0[:cols], v1[:cols], v0[cols:], v1[cols:]], 0)
+            term = dot3(v2, jnp.concatenate(his, 1), jnp.concatenate(los, 1), NT)
             total = term if total is None else total + term
-        out[:, pl.ds(pl.multiple_of(l * 256, 256), 256)] = total * (1.0 / 16.0)
+        total = total * (1.0 / 16.0)
+        a, b = total[:cols], total[cols:]
+        nk[t] = jnp.where(wide, a, b)
+        ns[t] = jnp.where(wide, b, a)
+        result(t).start()
         return carry
 
     for copy in get_lists:
         copy.wait()
-    ahead = jnp.where(z < 4, AHEAD, 0)
-
-    @pl.when(z < 4)
-    def _():
-        take_points()
-
-    lax.fori_loop(0, ahead, near, 0)
-
+    pass_on()
     total = contrib
     for k in range(1, 8):
         remote(sc, zb.at[k], z_send.at[k], z_recv.at[k], d, o).wait_recv()
@@ -303,7 +339,6 @@
     remote(sn.at[o], en.at[o, 1], n_send.at[2, o], n_recv.at[1, o], d, o).wait_recv()
     for copy in (get_lcp, get_ncp):
         copy.wait()
-    first = jnp.full((cols, 128), c, jnp.int32) == 0
 
     def keep(i, both):
         a, b = both[:cols], both[cols:]
@@ -320,11 +355,8 @@
             rows = pl.ds(j * 128 + h * 64, 64)
             tth[rows], ttl[rows] = split(tcp[h, j])
 
-    @pl.when(z >= 4)
-    def _():
-        take_points()
-
-    lax.fori_loop(ahead, 8, near, 0)
+    take_points()
+    lax.fori_loop(0, 4, near, 0)
 
     remote(sx, rx, x_send.at[0], x_recv.at[0], d, o).wait_recv()
     for k in range(1, 16):
@@ -336,15 +368,32 @@
     for l in range(leaves):
         leaf_local = ox[l] + rx[l] + dot3(node2, lth[l], ltl[l], NT)
         far = dot3(stacked(leaf_local), bh[l], bl[l], NT)
-        out[:, l * 256 : (l + 1) * 256] = out[:, l * 256 : (l + 1) * 256] + far
+        out[:, l * 256 : (l + 1) * 256] = far
+    for t in range(4):
+        result(t).wait_recv()
+    for l in range(leaves):
+        t, span = l % 4, slice(l * 256, (l + 1) * 256)
+        close = jnp.where(wide, nk[t], nr[t]) if l < 4 else jnp.where(wide, nr[t], nk[t])
+        out[:, span] = out[:, span] + close
     for copy in sends:
         copy.wait_send()
     for q, leaf, there, _ in sides:
 
         @pl.when(there)
         def _(q=q, leaf=leaf):
-            for copy in (*points_to(q, leaf), *moments_to(q, leaf)):
+            points = [coords_to(q, leaf), columns_to(q, leaf, 0), columns_to(q, leaf, 1)]
+            for copy in (*points, *moments_to(q, leaf)):
                 copy.wait_send()
+
+    for q, _, _, there in sides:
+
+        @pl.when(there)
+        def _(q=q):
+            forward(q).wait_send()
+            forward_coords(q, c).wait_send()
+
+    for t in range(4):
+        result(t).wait_send()
 
 
 def body(
@@ -357,7 +406,7 @@
     dma = pltpu.SemaphoreType.DMA
     return pl.pallas_call(
         kernel,
-        out_shape=jax.ShapeDtypeStruct(values.shape, F32),
+        out_shape=pltpu.VMEM(values.shape, F32),
         in_specs=[any_ref] * 12,
         out_specs=vmem,
         scratch_shapes=[
@@ -369,7 +418,11 @@
             pltpu.VMEM((cols, 2048), F32),
             pltpu.VMEM((2, cols, 2048), F32),
             pltpu.VMEM((25, 8, 128), F32),
-            pltpu.VMEM((25, 2 * cols, 256), BF16),
+            pltpu.VMEM((3, cols, 2048), F32),
+            pltpu.VMEM((2, 25, 2 * cols, 256), BF16),
+            pltpu.VMEM((4, cols, 256), F32),
+            pltpu.VMEM((4, cols, 256), F32),
+            pltpu.VMEM((4, cols, 256), F32),
             pltpu.VMEM((3, 256, 128), F32),
             pltpu.VMEM((2, 25, 8, 128), F32),
             pltpu.VMEM((2, 4, 8, 128), F32),
@@ -397,10 +450,10 @@
             pltpu.VMEM((9, cols, 128), F32),
             pltpu.VMEM((9, cols, 128), F32),
             dma((13,)),
-            dma((2,)), dma((2,)), dma((2,)), dma((2,)),
+            dma((2, 2)), dma((2, 2)), dma((2,)), dma((2,)),
             dma((3, 2)), dma((3, 2)), dma((3, 2)), dma((3, 2)),
             dma((8,)), dma((8,)), dma((16,)), dma((16,)),
-            dma((2,)), dma((2,)), pltpu.SemaphoreType.REGULAR((9,)),
+            dma((2,)), dma((2,)), dma((3,)), dma((3,)), dma((2,)), dma((2,)), dma((4,)), dma((4,)), pltpu.SemaphoreType.REGULAR((9,)),
         ],
         compiler_params=pltpu.CompilerParams(collective_id=0, has_side_effects=True),
     )(

time: 31.4 us -> 26.6 us (0.85)
  the two profiles are of different devices: /device:TPU:2 before, /device:TPU:3 now
where the time goes in v4:
time: 26.6 us; the launch traced here: 26.5 us
  Pallas kernels  25.8 us (97%)
  local copies, waits for them, and re-layouts  0.66 us (2%)
    pallas_call x1, Pallas kernels, body(): pl.pallas_call(kernel, out_shape=pltpu.VMEM(values.shape, F32), in_specs=...  25.8 us
    unnamed x1, local copies, waits for them, and re-layouts  0.66 us

profile of v4, /device:TPU:3, one launch (start us, length us, event | category | flops | bytes accessed | tf_op | source)
XLA Modules:
  0.0 26.5 jit_solution(5843727713970491556)
XLA Ops:
  0.0 25.8 %shard_map.118 = f32[16,2048]{1,0:T(8,128)S(1)} custom-call(s32[8,8]{1,0:T(8,128)} %near_hbm.1, s32[8,8]{1,0:T(8,128)} %leaf_hbm.1, s32[1,2]{1,0:T(1,128)} %node_hbm.1, s32[4,16]{1,0:T(4,128)} %bitcast.1, f32[3,2048]{1,0:T(4,128)} %coords_hbm.1, f32[16,2048]{1,0:T(8,128)} %values_hbm.1, f32[8,256,128]{2,1,0:T(8,128)} %basis_hbm.1, f32[8,128,128]{2,1,0:T(8,128)} %ltr_hbm.1, ...), custom_call_target="tpu_custom_call" | custom-call | tf_op jit(solution)/shard_map/pallas_call | solution.py:407
  25.8 0.7 %copy.14 = f32[16,2048]{1,0:T(8,128)} copy(f32[16,2048]{1,0:T(8,128)S(1)} %shard_map.118) | data formatting | bytes 262144

commit v5 on v4

--- a/solution.py
+++ b/solution.py
@@ -42,7 +42,7 @@
     basis, ltr, ntr, lcp, ncp, tcp, bh, bl, lth, ltl, nth, ntl, tth, ttl,
     ox, sx, rx,
     local_sem, v_send, v_recv, c_send, c_recv, m_send, m_recv, n_send, n_recv,
-    z_send, z_recv, t_send, t_recv, x_send, x_recv, f_send, f_recv, g_send, g_recv, r_send, r_recv, tokens,
+    z_send, z_recv, t_send, t_recv, x_send, x_recv, f_send, f_recv, g_send, g_recv, r_send, r_recv, tokens, answers,
 ):
     leaves, chips = 8, 128
     cols = vals.shape[0]
@@ -88,14 +88,45 @@
     sides = ((0, after, no_after == 0, no_before == 0), (1, before, no_before == 0, no_after == 0))
 
     greet(d, o)
-    for leaf in (z_up, z_down, x_up, x_down, y_up, y_down):
-        greet(leaf, c)
+    greet(z_up, c)
+    greet(z_down, c)
     for _, leaf, there, _ in sides:
 
         @pl.when(there)
         def _(leaf=leaf):
             greet(leaf, 0)
             greet(leaf, 1)
+
+    def relation(mine, theirs, leaf, farther):
+        return mine, theirs, leaf, farther, jnp.logical_not(farther)
+
+    relations = (
+        relation(0, 1, x_up, x < 3),
+        relation(1, 0, x_down, x == 0),
+        relation(2, 3, y_up, y < 3),
+        relation(3, 2, y_down, y == 0),
+    )
+    for _, _, leaf, far, _ in relations:
+
+        @pl.when(far)
+        def _(leaf=leaf):
+            greet(leaf, c)
+
+    greeters = sum(near.astype(jnp.int32) for *_, near in relations)
+
+    def answer():
+        for _, theirs, leaf, _, near in relations:
+
+            @pl.when(near)
+            def _(theirs=theirs, leaf=leaf):
+                pl.semaphore_signal(answers.at[theirs], inc=1, device_id=(leaf, c), device_id_type=MESH)
+
+    def known():
+        for mine, _, _, far, _ in relations:
+
+            @pl.when(far)
+            def _(mine=mine):
+                pl.semaphore_wait(answers.at[mine], 1)
 
     def token(i, leaf):
         pl.semaphore_signal(tokens.at[i], inc=1, device_id=(leaf, c), device_id_type=MESH)
@@ -146,7 +177,7 @@
             cs[leaves + l, 3 * h : 3 * h + 3, :] = coords[:, start : start + 128]
         cs[leaves + l, 6:8, :] = zero8[:2]
     get_values.wait()
-    pl.semaphore_wait(barrier, 11 - 2 * no_after - 2 * no_before)
+    pl.semaphore_wait(barrier, 7 - 2 * no_after - 2 * no_before + greeters)
     for q, leaf, there, _ in sides:
 
         @pl.when(there)
@@ -158,7 +189,7 @@
     send(vals, rv.at[2], f_send.at[2], f_recv.at[2], d, o)
     token(0, z_up)
     token(3, z_down)
-    token(5, x_down)
+    answer()
 
     for l in range(leaves):
         vs[c, leaves + l] = stacked(vals[:, l * 256 : (l + 1) * 256])
@@ -181,9 +212,6 @@
     token(1, z_up)
     heard(3)
     token(4, z_down)
-    heard(5)
-    token(6, y_up)
-    token(8, y_down)
     heard(1)
     token(2, z_up)
     heard(4, 2)
@@ -196,6 +224,8 @@
         a, b = x[:8], x[8:]
         return jnp.where(low, a, pltpu.roll(b, 64, 1)) if h == 0 else jnp.where(low, pltpu.roll(a, 64, 1), b)
 
+    known()
+    token(5, x_down)
     for h in range(2):
         sn[h] = half(node, h)
         for l in range(leaves):
@@ -214,6 +244,9 @@
     em[c, own] = sm[c]
     en[c, 1] = sn[c]
 
+    heard(5)
+    token(6, y_up)
+    token(8, y_down)
     heard(6)
     token(7, y_up)
     cs[24] = zero8
@@ -453,7 +486,7 @@
             dma((2, 2)), dma((2, 2)), dma((2,)), dma((2,)),
             dma((3, 2)), dma((3, 2)), dma((3, 2)), dma((3, 2)),
             dma((8,)), dma((8,)), dma((16,)), dma((16,)),
-            dma((2,)), dma((2,)), dma((3,)), dma((3,)), dma((2,)), dma((2,)), dma((4,)), dma((4,)), pltpu.SemaphoreType.REGULAR((9,)),
+            dma((2,)), dma((2,)), dma((3,)), dma((3,)), dma((2,)), dma((2,)), dma((4,)), dma((4,)), pltpu.SemaphoreType.REGULAR((9,)), pltpu.SemaphoreType.REGULAR((4,)),
         ],
         compiler_params=pltpu.CompilerParams(collective_id=0, has_side_effects=True),
     )(

time: 26.6 us -> 25.9 us (0.974)
  the two profiles are of different devices: /device:TPU:3 before, /device:TPU:7 now
where the time goes in v5:
time: 25.9 us; the launch traced here: 25.8 us
  Pallas kernels  25.1 us (97%)
  local copies, waits for them, and re-layouts  0.66 us (3%)
    pallas_call x1, Pallas kernels, body(): pl.pallas_call(kernel, out_shape=pltpu.VMEM(values.shape, F32), in_specs=...  25.1 us
    unnamed x1, local copies, waits for them, and re-layouts  0.66 us

profile of v5, /device:TPU:7, one launch (start us, length us, event | category | flops | bytes accessed | tf_op | source)
XLA Modules:
  0.0 25.8 jit_solution(9084758582042657303)
XLA Ops:
  0.0 25.1 %shard_map.118 = f32[16,2048]{1,0:T(8,128)S(1)} custom-call(s32[8,8]{1,0:T(8,128)} %near_hbm.1, s32[8,8]{1,0:T(8,128)} %leaf_hbm.1, s32[1,2]{1,0:T(1,128)} %node_hbm.1, s32[4,16]{1,0:T(4,128)} %bitcast.1, f32[3,2048]{1,0:T(4,128)} %coords_hbm.1, f32[16,2048]{1,0:T(8,128)} %values_hbm.1, f32[8,256,128]{2,1,0:T(8,128)} %basis_hbm.1, f32[8,128,128]{2,1,0:T(8,128)} %ltr_hbm.1, ...), custom_call_target="tpu_custom_call" | custom-call | tf_op jit(solution)/shard_map/pallas_call | solution.py:440
  25.2 0.7 %copy.14 = f32[16,2048]{1,0:T(8,128)} copy(f32[16,2048]{1,0:T(8,128)S(1)} %shard_map.118) | data formatting | bytes 262144

commit v6 on v5

--- a/solution.py
+++ b/solution.py
@@ -208,39 +208,42 @@
     nth[...], ntl[...] = split(ntr[0])
     contrib = dot3(stacked(node), nth[...], ntl[...], NN)
     sc[...] = contrib
+    low = lax.broadcasted_iota(jnp.int32, (8, 128), 1) < 64
+
+    def half(x, h):
+        a, b = x[:8], x[8:]
+        return jnp.where(low, a, pltpu.roll(b, 64, 1)) if h == 0 else jnp.where(low, pltpu.roll(a, 64, 1), b)
+
+    for h in range(2):
+        sn[h] = half(node, h)
+        for l in range(leaves):
+            sm[h, l] = half(moments[l], h)
+    for q, leaf, there, _ in sides:
+
+        @pl.when(there)
+        def _(q=q, leaf=leaf):
+            for copy in moments_to(q, leaf):
+                copy.start()
+
     heard(0)
     token(1, z_up)
     heard(3)
     token(4, z_down)
     heard(1)
     token(2, z_up)
-    heard(4, 2)
-    for k in range(1, 8):
+    heard(2)
+    for k in (4, 5, 6, 7, 1):
         send(sc, zb.at[k], z_send.at[k], z_recv.at[k], g * 8 + lax.rem(z + k, 8), c)
-
-    low = lax.broadcasted_iota(jnp.int32, (8, 128), 1) < 64
-
-    def half(x, h):
-        a, b = x[:8], x[8:]
-        return jnp.where(low, a, pltpu.roll(b, 64, 1)) if h == 0 else jnp.where(low, pltpu.roll(a, 64, 1), b)
-
+    heard(4)
+    for k in (2, 3):
+        send(sc, zb.at[k], z_send.at[k], z_recv.at[k], g * 8 + lax.rem(z + k, 8), c)
+
+    send(sm.at[o], em.at[c, own], m_send.at[2, o], m_recv.at[1, c], d, o)
+    send(sn.at[o], en.at[c, 1], n_send.at[2, o], n_recv.at[1, c], d, o)
+    get_tcp.wait()
+    send(tcp.at[c], tcp.at[c], x_send.at[1], x_recv.at[1], d, o)
     known()
     token(5, x_down)
-    for h in range(2):
-        sn[h] = half(node, h)
-        for l in range(leaves):
-            sm[h, l] = half(moments[l], h)
-    get_tcp.wait()
-    send(tcp.at[c], tcp.at[c], x_send.at[1], x_recv.at[1], d, o)
-    send(sm.at[o], em.at[c, own], m_send.at[2, o], m_recv.at[1, c], d, o)
-    send(sn.at[o], en.at[c, 1], n_send.at[2, o], n_recv.at[1, c], d, o)
-    for q, leaf, there, _ in sides:
-
-        @pl.when(there)
-        def _(q=q, leaf=leaf):
-            for copy in moments_to(q, leaf):
-                copy.start()
-
     em[c, own] = sm[c]
     en[c, 1] = sn[c]
 

time: 25.9 us -> 25.1 us (0.969)
  the two profiles are of different devices: /device:TPU:7 before, /device:TPU:1 now
where the time goes in v6:
time: 25.1 us; the launch traced here: 24.8 us
  Pallas kernels  24.2 us (96%)
  local copies, waits for them, and re-layouts  0.66 us (3%)
    pallas_call x1, Pallas kernels, body(): pl.pallas_call(kernel, out_shape=pltpu.VMEM(values.shape, F32), in_specs=...  24.2 us
    unnamed x1, local copies, waits for them, and re-layouts  0.66 us

profile of v6, /device:TPU:1, one launch (start us, length us, event | category | flops | bytes accessed | tf_op | source)
XLA Modules:
  0.0 24.8 jit_solution(14523058373706487363)
XLA Ops:
  0.0 24.2 %shard_map.118 = f32[16,2048]{1,0:T(8,128)S(1)} custom-call(s32[8,8]{1,0:T(8,128)} %near_hbm.1, s32[8,8]{1,0:T(8,128)} %leaf_hbm.1, s32[1,2]{1,0:T(1,128)} %node_hbm.1, s32[4,16]{1,0:T(4,128)} %bitcast.1, f32[3,2048]{1,0:T(4,128)} %coords_hbm.1, f32[16,2048]{1,0:T(8,128)} %values_hbm.1, f32[8,256,128]{2,1,0:T(8,128)} %basis_hbm.1, f32[8,128,128]{2,1,0:T(8,128)} %ltr_hbm.1, ...), custom_call_target="tpu_custom_call" | custom-call | tf_op jit(solution)/shard_map/pallas_call | solution.py:443
  24.2 0.7 %copy.14 = f32[16,2048]{1,0:T(8,128)} copy(f32[16,2048]{1,0:T(8,128)S(1)} %shard_map.118) | data formatting | bytes 262144

commit v7 on v6

--- a/solution.py
+++ b/solution.py
@@ -170,26 +170,31 @@
             )
         ]
 
+    pl.semaphore_wait(barrier, 7 - 2 * no_after - 2 * no_before + greeters)
+    token(0, z_up)
+    token(3, z_down)
+    answer()
+    get_values.wait()
+    for q, leaf, there, _ in sides:
+
+        @pl.when(there)
+        def _(q=q, leaf=leaf):
+            columns_to(q, leaf, 0).start()
+            columns_to(q, leaf, 1).start()
+
     get_coords.wait()
     for l in range(leaves):
         for h in range(2):
             start = l * 256 + h * 128
             cs[leaves + l, 3 * h : 3 * h + 3, :] = coords[:, start : start + 128]
         cs[leaves + l, 6:8, :] = zero8[:2]
-    get_values.wait()
-    pl.semaphore_wait(barrier, 7 - 2 * no_after - 2 * no_before + greeters)
     for q, leaf, there, _ in sides:
 
         @pl.when(there)
         def _(q=q, leaf=leaf):
             coords_to(q, leaf).start()
-            columns_to(q, leaf, 0).start()
-            columns_to(q, leaf, 1).start()
 
     send(vals, rv.at[2], f_send.at[2], f_recv.at[2], d, o)
-    token(0, z_up)
-    token(3, z_down)
-    answer()
 
     for l in range(leaves):
         vs[c, leaves + l] = stacked(vals[:, l * 256 : (l + 1) * 256])
@@ -346,8 +351,9 @@
         total = total + zb[k]
     st[...] = total
     heard(8, 7)
-    for k in range(1, 16):
-        send(st, tb.at[g], t_send.at[k], t_recv.at[k], lax.rem(g + k, 16) * 8 + z, c)
+    far_first = sorted(range(1, 16), key=lambda k: -(min(k // 4, 4 - k // 4) + min(k % 4, 4 - k % 4)))
+    for k in far_first:
+        send(st, tb.at[g], t_send.at[k], t_recv.at[k], chip(x + k // 4, y + k % 4, z), c)
     tb[g] = total
 
     def paired(load, i, j):

time: 25.1 us -> 25.1 us (level)
  no operation moved by 1% of the time
where the time goes in v7:
time: 25.1 us; the launch traced here: 24.7 us
  Pallas kernels  24 us (96%)
  local copies, waits for them, and re-layouts  0.66 us (3%)
    pallas_call x1, Pallas kernels, body(): pl.pallas_call(kernel, out_shape=pltpu.VMEM(values.shape, F32), in_specs=...  24 us
    unnamed x1, local copies, waits for them, and re-layouts  0.66 us

profile of v7, /device:TPU:1, one launch (start us, length us, event | category | flops | bytes accessed | tf_op | source)
XLA Modules:
  0.0 24.7 jit_solution(13246113682814568234)
XLA Ops:
  0.0 24.0 %shard_map.118 = f32[16,2048]{1,0:T(8,128)S(1)} custom-call(s32[8,8]{1,0:T(8,128)} %near_hbm.1, s32[8,8]{1,0:T(8,128)} %leaf_hbm.1, s32[1,2]{1,0:T(1,128)} %node_hbm.1, s32[4,16]{1,0:T(4,128)} %bitcast.1, f32[3,2048]{1,0:T(4,128)} %coords_hbm.1, f32[16,2048]{1,0:T(8,128)} %values_hbm.1, f32[8,256,128]{2,1,0:T(8,128)} %basis_hbm.1, f32[8,128,128]{2,1,0:T(8,128)} %ltr_hbm.1, ...), custom_call_target="tpu_custom_call" | custom-call | tf_op jit(solution)/shard_map/pallas_call | solution.py:449
  24.0 0.7 %copy.14 = f32[16,2048]{1,0:T(8,128)} copy(f32[16,2048]{1,0:T(8,128)S(1)} %shard_map.118) | data formatting | bytes 262144

commit v8 on v7

--- a/solution.py
+++ b/solution.py
@@ -194,7 +194,7 @@
         def _(q=q, leaf=leaf):
             coords_to(q, leaf).start()
 
-    send(vals, rv.at[2], f_send.at[2], f_recv.at[2], d, o)
+    send(vals, rv.at[2], f_send.at[2, 0], f_recv.at[2, 0], d, o)
 
     for l in range(leaves):
         vs[c, leaves + l] = stacked(vals[:, l * 256 : (l + 1) * 256])
@@ -267,8 +267,9 @@
     def source(v, first, none):
         return jnp.where(v >= 0, jnp.clip(v - first, 0, none - 1), none)
 
-    def forward(q):
-        return remote(ev.at[q], rv.at[q], f_send.at[q], f_recv.at[q], d, o)
+    def forward(q, part):
+        rows = pl.ds(part * 8, 8)
+        return remote(ev.at[q, rows], rv.at[q, rows], f_send.at[q, part], f_recv.at[q, part], d, o)
 
     def forward_coords(q, core):
         land = cs.at[pl.ds(16 * q + 4 * core, 4)]
@@ -279,11 +280,11 @@
 
             @pl.when(there)
             def _(q=q, leaf=leaf):
+                for part in range(2):
+                    columns_to(q, leaf, part).wait_recv()
+                    forward(q, part).start()
                 coords_to(q, leaf).wait_recv()
                 forward_coords(q, c).start()
-                for part in range(2):
-                    columns_to(q, leaf, part).wait_recv()
-                forward(q).start()
 
     def take_points():
         for q, _, _, there in sides:
@@ -293,7 +294,7 @@
                 for l in range(leaves):
                     vs[c, 16 * q + l] = stacked(ev[q, :, l * 256 : (l + 1) * 256])
 
-        remote(vals, rv.at[2], f_send.at[2], f_recv.at[2], d, o).wait_recv()
+        remote(vals, rv.at[2], f_send.at[2, 0], f_recv.at[2, 0], d, o).wait_recv()
         for l in range(leaves):
             vs[o, leaves + l] = stacked(rv[2, :, l * 256 : (l + 1) * 256])
         for q, _, _, there in sides:
@@ -301,7 +302,8 @@
             @pl.when(there)
             def _(q=q):
                 forward_coords(q, o).wait_recv()
-                forward(q).wait_recv()
+                forward(q, 0).wait_recv()
+                forward(q, 1).wait_recv()
                 for l in range(leaves):
                     vs[o, 16 * q + l] = stacked(rv[q, :, l * 256 : (l + 1) * 256])
 
@@ -431,7 +433,8 @@
 
         @pl.when(there)
         def _(q=q):
-            forward(q).wait_send()
+            forward(q, 0).wait_send()
+            forward(q, 1).wait_send()
             forward_coords(q, c).wait_send()
 
     for t in range(4):
@@ -495,7 +498,7 @@
             dma((2, 2)), dma((2, 2)), dma((2,)), dma((2,)),
             dma((3, 2)), dma((3, 2)), dma((3, 2)), dma((3, 2)),
             dma((8,)), dma((8,)), dma((16,)), dma((16,)),
-            dma((2,)), dma((2,)), dma((3,)), dma((3,)), dma((2,)), dma((2,)), dma((4,)), dma((4,)), pltpu.SemaphoreType.REGULAR((9,)), pltpu.SemaphoreType.REGULAR((4,)),
+            dma((2,)), dma((2,)), dma((3, 2)), dma((3, 2)), dma((2,)), dma((2,)), dma((4,)), dma((4,)), pltpu.SemaphoreType.REGULAR((9,)), pltpu.SemaphoreType.REGULAR((4,)),
         ],
         compiler_params=pltpu.CompilerParams(collective_id=0, has_side_effects=True),
     )(

time: 25.1 us -> 25.1 us (level)
  no operation moved by 1% of the time
where the time goes in v8:
time: 25.1 us; the launch traced here: 24.8 us
  Pallas kernels  24.1 us (96%)
  local copies, waits for them, and re-layouts  0.66 us (3%)
    pallas_call x1, Pallas kernels, body(): pl.pallas_call(kernel, out_shape=pltpu.VMEM(values.shape, F32), in_specs=...  24.1 us
    unnamed x1, local copies, waits for them, and re-layouts  0.66 us

profile of v8, /device:TPU:1, one launch (start us, length us, event | category | flops | bytes accessed | tf_op | source)
XLA Modules:
  0.0 24.8 jit_solution(4752924005288868949)
XLA Ops:
  0.0 24.1 %shard_map.118 = f32[16,2048]{1,0:T(8,128)S(1)} custom-call(s32[8,8]{1,0:T(8,128)} %near_hbm.1, s32[8,8]{1,0:T(8,128)} %leaf_hbm.1, s32[1,2]{1,0:T(1,128)} %node_hbm.1, s32[4,16]{1,0:T(4,128)} %bitcast.1, f32[3,2048]{1,0:T(4,128)} %coords_hbm.1, f32[16,2048]{1,0:T(8,128)} %values_hbm.1, f32[8,256,128]{2,1,0:T(8,128)} %basis_hbm.1, f32[8,128,128]{2,1,0:T(8,128)} %ltr_hbm.1, ...), custom_call_target="tpu_custom_call" | custom-call | tf_op jit(solution)/shard_map/pallas_call | solution.py:452
  24.1 0.7 %copy.14 = f32[16,2048]{1,0:T(8,128)} copy(f32[16,2048]{1,0:T(8,128)S(1)} %shard_map.118) | data formatting | bytes 262144
